TPU v7x, 1024 devices: a whole 4x8x16 slice. The times are simulated.
1024 devices in a mesh: row: 32 (over z, core), col: 32 (over x, y).
Axes of the slice: x: 4, y: 8, z: 16, core: 2. Of those that a mesh axis runs over, the one named last changes fastest.
Arguments:
- matrix: float32 [20480, 20480], P('row', 'col'), may hold values from -16 to 16, as said below
Outputs:
- reduced: float32 [20480, 20480], P('row', 'col')
Inputs may be any that keep to these rules, and one draw needn't show every extreme that they name: matrix is exactly symmetric.
All inputs are finite; a program needn't handle non-finite values.
Results may differ from a plain program's by a relative error of at most 0.0015.
Values may be sent and summed in bfloat16 or wider, within the bound.
A program may use at most 32 MiB of HBM per device.

v0:
```python
import jax
import jax.numpy as jnp
from jax import lax
from jax.sharding import PartitionSpec as P

PW = 64


HIGHEST = lax.Precision.HIGHEST


def spread(value, axis, source):
    kept = jnp.where(lax.axis_index(axis) == source, value, 0).astype(value.dtype)
    return lax.psum(kept, axis)


def select_rows(starts, count_rows, upper_factor):
    offsets = starts + jnp.arange(count_rows, dtype=jnp.int32) - PW
    picker = (offsets[:, None] == jnp.arange(PW, dtype=jnp.int32)[None, :]).astype(jnp.float32)
    return jnp.dot(picker, upper_factor, precision=HIGHEST, preferred_element_type=jnp.float32)


def contract_rows(first, second, precise):
    if precise:
        return lax.dot_general(
            first,
            second,
            (((0,), (0,)), ((), ())),
            precision=HIGHEST,
            preferred_element_type=jnp.float32,
        )
    return lax.dot_general(
        first, second, (((0,), (0,)), ((), ())), preferred_element_type=jnp.float32
    )


def make_update(images, basis_half, core_inverse, middle):
    basis_wide = basis_half.astype(jnp.float32)
    first_term = jnp.dot(
        images, core_inverse, precision=HIGHEST, preferred_element_type=jnp.float32
    )
    second_term = jnp.dot(basis_wide, middle, precision=HIGHEST, preferred_element_type=jnp.float32)
    return (first_term - 0.5 * second_term).astype(jnp.bfloat16)


def on_device(matrix):
    row_count, col_count = matrix.shape
    row_index = lax.axis_index("row")
    col_index = lax.axis_index("col")
    row_start = row_index * row_count
    col_start = col_index * col_count
    global_rows = row_start + jnp.arange(row_count, dtype=jnp.int32)
    global_cols = col_start + jnp.arange(col_count, dtype=jnp.int32)
    left_part = jnp.where((global_rows >= PW)[:, None], matrix[:, :PW], jnp.float32(0.0))
    gram_term = jnp.where(
        col_index == 0, contract_rows(left_part, left_part, True), jnp.float32(0.0)
    )
    top_term = jnp.where(
        (row_index == 0) & (col_index == 0), matrix[PW : 2 * PW, :PW], jnp.float32(0.0)
    )
    gram_matrix, top_block = lax.psum((gram_term, top_term), ("row", "col"))
    upper_factor = jnp.linalg.cholesky(gram_matrix).T
    shifted_top = top_block + upper_factor
    coupling = contract_rows(shifted_top, upper_factor, True)
    normal_matrix = jnp.dot(
        coupling, coupling.T, precision=HIGHEST, preferred_element_type=jnp.float32
    )
    lower_factor = jnp.linalg.cholesky(normal_matrix)
    halfway = lax.linalg.triangular_solve(lower_factor, coupling, left_side=True, lower=True)
    solved = lax.linalg.triangular_solve(
        lower_factor, halfway, left_side=True, lower=True, transpose_a=True
    )
    core_inverse = solved.T
    local_rows = (left_part + select_rows(row_start, row_count, upper_factor)).astype(jnp.bfloat16)
    row_basis = spread(local_rows, "col", 0)
    top_rows = matrix[:PW, :]
    local_cols = jnp.where(
        (global_cols >= PW)[:, None], top_rows.T, jnp.float32(0.0)
    ) + select_rows(col_start, col_count, upper_factor)
    col_basis = spread(local_cols.astype(jnp.bfloat16), "row", 0)
    matrix_half = matrix.astype(jnp.bfloat16)
    row_images = lax.psum(
        jnp.dot(matrix_half, col_basis, preferred_element_type=jnp.float32), "col"
    )
    projection_term = contract_rows(row_basis.astype(jnp.float32), row_images, True)
    col_partial = contract_rows(matrix_half, row_basis, False)
    col_images, projection = lax.psum((col_partial, projection_term), "row")
    middle = jnp.dot(
        jnp.dot(core_inverse.T, projection, precision=HIGHEST, preferred_element_type=jnp.float32),
        core_inverse,
        precision=HIGHEST,
        preferred_element_type=jnp.float32,
    )
    row_update = make_update(row_images, row_basis, core_inverse, middle)
    col_update = make_update(col_images, col_basis, core_inverse, middle)
    left_side = jnp.concatenate([row_basis, row_update], axis=1)
    right_side = jnp.concatenate([col_update, col_basis], axis=1)
    product = lax.dot_general(
        left_side, right_side, (((1,), (1,)), ((), ())), preferred_element_type=jnp.float32
    )
    return matrix - product


def solution(mesh):
    placed = (P("row", "col"),)
    return jax.shard_map(
        on_device, mesh=mesh, in_specs=placed, out_specs=P("row", "col"), check_vma=False
    )
```

profile of v0, /device:TPU:2, one launch (start us, length us, event | category | flops | bytes accessed | tf_op | source)
XLA Modules:
  0.0 908.1 jit_solution(7992975073621610092)
XLA Ops:
  6.6 1.1 slice.21
  7.7 0.8 slice_select_fusion
  8.6 0.3 convolution_select_fusion
  8.9 135.5 %all-reduce = (f32[64,64]{1,0:T(8,128)S(1)}, f32[64,64]{1,0:T(8,128)S(1)}) all-reduce(f32[64,64]{1,0:T(8,128)S(1)} %convolution_select_fusion, f32[64,64]{1,0:T(8,128)S(1)} %slice_select_fusion), channel_id=1, replica_groups=mesh['row'=32,'col'=32] {'row','col'}, use_global_device_ids=true, to_apply=%region_0.1 | all-reduce | flops 8192 | bytes 65536 | tf_op jit(solution)/shard_map/psum | solution.py:61
  144.5 5.9 cholesky.44
  150.6 0.7 compare_reduce_fusion.1
  151.3 1.8 fusion.4
  153.2 1.8 fusion.5
  155.0 0.9 fusion.25
  156.3 5.8 cholesky.55
  162.1 0.7 compare_reduce_fusion
  162.9 0.7 fusion.19
  163.6 4.9 custom-call.7
  168.9 168.2 %all-reduce.8.cloned.1.call-done = bf16[640,64]{0,1:T(8,128)(2,1)} async-done(((bf16[640,64]{0,1:T(8,128)(2,1)}), bf16[640,64]{0,1:T(8,128)(2,1)}) %all-reduce.8.cloned.1.call-update) | async-done | bytes 81936 | tf_op jit(solution)/shard_map/psum | solution.py:14
  337.1 1.9 convolution_bitcast_fusion.1
  339.1 170.6 %all-reduce.6.cloned.1.call-done = bf16[640,64]{0,1:T(8,128)(2,1)} async-done(((bf16[640,64]{0,1:T(8,128)(2,1)}), bf16[640,64]{0,1:T(8,128)(2,1)}) %all-reduce.6.cloned.1.call-update) | async-done | bytes 81936 | tf_op jit(solution)/shard_map/psum | solution.py:14
  509.8 1.9 convolution_bitcast_fusion
  511.7 176.6 %all-reduce.10.cloned.1.call-done = f32[640,64]{0,1:T(8,128)} async-done(((f32[640,64]{0,1:T(8,128)}), f32[640,64]{0,1:T(8,128)}) %all-reduce.10.cloned.1.call-update) | async-done | bytes 163856 | tf_op jit(solution)/shard_map/psum | solution.py:82
  688.2 1.2 fusion.49
  689.4 92.6 %psum.54 = f32[64,64]{1,0:T(8,128)S(1)} all-reduce(f32[64,64]{1,0:T(8,128)S(1)} %fusion.49), channel_id=1, replica_groups=mesh['row'=32,'col'=32] {'row'}, use_global_device_ids=true, to_apply=%region_7.9 | all-reduce | flops 4096 | bytes 32768 | tf_op jit(solution)/shard_map/psum | solution.py:87
  782.6 1.2 fusion.2
  784.1 114.7 %all-reduce.12.cloned.1.call-done = f32[640,64]{0,1:T(8,128)} async-done(((f32[640,64]{0,1:T(8,128)}), f32[640,64]{0,1:T(8,128)}) %all-reduce.12.cloned.1.call-update) | async-done | bytes 163856 | tf_op jit(solution)/shard_map/psum | solution.py:87
  898.8 1.2 fusion.3
  900.0 1.6 convolution_subtract_fusion
  (34 shorter events, 2.3 us)
Async XLA Ops:
  6.5 144.8 %copy-start = (f32[640,640]{1,0:T(8,128)S(1)}, f32[640,640]{1,0:T(8,128)}, u32[]{:S(2)}) copy-start(f32[640,640]{1,0:T(8,128)} %param.2) | copy-start | bytes 4915204
  6.5 330.6 %all-reduce.8.cloned.1.call-start = ((), (), s32[]{:S(2)}) async-start(), calls=%async_computation.1 | async-start | bytes 163840 | tf_op jit(solution)/shard_map/psum | solution.py:14
  153.1 356.6 %all-reduce.6.cloned.1.call-start = ((), (), s32[]{:S(2)}) async-start(), calls=%async_computation | async-start | bytes 163840 | tf_op jit(solution)/shard_map/psum | solution.py:14
  155.0 533.2 %all-reduce.10.cloned.1.call-start = ((), (), s32[]{:S(2)}) async-start(), calls=%async_computation.2 | async-start | bytes 327680 | tf_op jit(solution)/shard_map/psum | solution.py:82
  339.1 444.7 %copy-start.2 = (bf16[640,64]{0,1:T(8,128)(2,1)S(1)}, bf16[640,64]{0,1:T(8,128)(2,1)}, u32[]{:S(2)}) copy-start(bf16[640,64]{0,1:T(8,128)(2,1)} %all-reduce.8.cloned.1.call-done) | copy-start | bytes 245764
  339.1 559.7 %all-reduce.12.cloned.1.call-start = ((), (), s32[]{:S(2)}) async-start(), calls=%async_computation.3 | async-start | bytes 327680 | tf_op jit(solution)/shard_map/psum | solution.py:87
  509.8 178.5 %copy-start.1 = (bf16[640,64]{0,1:T(8,128)(2,1)S(1)}, bf16[640,64]{0,1:T(8,128)(2,1)}, u32[]{:S(2)}) copy-start(bf16[640,64]{0,1:T(8,128)(2,1)} %all-reduce.6.cloned.1.call-done) | copy-start | bytes 245764
Sparse Core Ops, SparseCore 0:
  153.3 183.8 all-reduce.7
  340.6 169.1 all-reduce.5
  513.2 174.9 all-reduce.9
  690.4 208.3 all-reduce.11
where the time goes:
time: 909 us; the launch traced here: 908 us
  waiting for transfers between devices  630 us (69%)
  blocking collectives  228 us (25%)
  other arithmetic  19.7 us (2%)
  matrix products  15.2 us (2%)
  between operations  13.3 us (1%)
    psum x2, waiting for transfers between devices, spread(): return lax.psum(kept, axis)  339 us
    psum x1, waiting for transfers between devices, on_device(): lax.psum(jnp.dot(matrix_half, col_basis, preferred_element_type=jnp.float...  177 us
    psum x1, blocking collectives, on_device(): gram_matrix, top_block = lax.psum((gram_term, top_term), ('row', 'col'))  135 us
    psum x1, waiting for transfers between devices, on_device(): col_images, projection = lax.psum((col_partial, projection_term), 'row')  115 us
    psum x1, blocking collectives, on_device(): col_images, projection = lax.psum((col_partial, projection_term), 'row')  92.6 us
  transfers between devices with their start and end apart: 4, of which 4 were waited for; matrix products, arithmetic and copies ran while one was open for 2% of the time, Pallas kernels for 0%

commit v1 on v0

v1 whole, which is shorter than its diff:
```python
import functools

import jax
import jax.numpy as jnp
from jax import lax
from jax.experimental import pallas as pl
from jax.experimental.pallas import tpu as pltpu
from jax.sharding import PartitionSpec as P

PW = 64
HIGHEST = lax.Precision.HIGHEST
MESH = pl.DeviceIdType.MESH
F32 = jnp.float32
BF16 = jnp.bfloat16


def dot(first, second, dims, precision=None):
    return lax.dot_general(
        first, second, (dims, ((), ())), precision=precision, preferred_element_type=F32
    )


def far_first(count):
    return sorted(range(1, count), key=lambda d: -min(d, count - d))


def exchange(shape, a_ref, rowp_ref, colp_ref, gpart_ref,
             li_out, lj_out, zi_out, zj_out, g_out, k_out,
             li, lj, zp, zs, zr, zx, zi, zj, gs, gr, gx, g, kp, ks, kz, kc, kf, kk,
             send_z, recv_z, send_y, recv_y, send_x, recv_x, send_k, recv_k,
             send_b, recv_b, send_c, recv_c):
    nz, nx, ny = shape
    row, col = lax.axis_index("row"), lax.axis_index("col")
    z, c = row // 2, row % 2
    x, y = col // ny, col % ny
    partner = (z * 2 + 1 - c, col)

    def at_z(d):
        return (lax.rem(z + d, nz) * 2 + c, col)

    def at_y(d):
        return (row, x * ny + lax.rem(y + d, ny))

    def at_x(d):
        return (row, lax.rem(x + d, nx) * ny + y)

    def copy(src, dst, send, recv, where):
        return pltpu.make_async_remote_copy(
            src_ref=src, dst_ref=dst, send_sem=send, recv_sem=recv,
            device_id=where, device_id_type=MESH,
        )

    def got(ref, sem):
        copy(ref, ref, sem, sem, partner).wait_recv()

    def sent(ref, sem):
        copy(ref, ref, sem, sem, partner).wait_send()

    barrier = pltpu.get_barrier_semaphore()
    peers = [at_z(d) for d in range(1, nz)] + [at_y(d) for d in range(1, ny)]
    peers += [at_x(d) for d in range(1, nx)] + [partner]
    for peer in peers:
        pl.semaphore_signal(barrier, inc=1, device_id=peer, device_id_type=MESH)
    pl.semaphore_wait(barrier, len(peers))

    @pl.when(row == 0)
    def _():
        for d in far_first(nz):
            copy(colp_ref.at[0], lj.at[0], send_z.at[0, d], recv_b.at[0], at_z(d)).start()
        copy(colp_ref.at[0], lj.at[0], send_c.at[0], recv_b.at[0], partner).start()

    @pl.when(col == 0)
    def _():
        for d in far_first(ny):
            copy(rowp_ref.at[d], li.at[d], send_y.at[0, d], recv_b.at[3], at_y(d)).start()
        for d in range(1, nx):
            copy(rowp_ref.at[0], li.at[0], send_x.at[0, d], recv_x.at[0, 0], at_x(d)).start()
        li[0] = rowp_ref[0]

    @pl.when(row == 0)
    def _():
        for d in far_first(ny):
            there = lax.rem(y + d, ny)
            copy(gpart_ref.at[there], gs.at[d], send_y.at[1, d], recv_y.at[1, d], at_y(d)).start()
        lj[...] = colp_ref[...]

    @pl.when((x == 0) & (y != 0))
    def _():
        got(li.at[y], recv_b.at[3])
        for d in range(1, nx):
            copy(li.at[y], li.at[y], send_x.at[0, d], recv_x.at[0, 0], at_x(d)).start()

    @pl.when(x != 0)
    def _():
        got(li.at[y], recv_x.at[0, 0])

    @pl.when(col == 0)
    def _():
        for d in far_first(ny):
            copy(rowp_ref.at[0], li.at[0], send_y.at[2, d], recv_y.at[2, d], at_y(d)).start()

    @pl.when(col != 0)
    def _():
        for d in far_first(ny):
            copy(li.at[y], li.at[y], send_y.at[2, d], recv_y.at[2, d], at_y(d)).start()

    @pl.when((row != 0) & (c == 0))
    def _():
        got(lj.at[0], recv_b.at[0])
        copy(lj.at[0], lj.at[0], send_c.at[0], recv_b.at[0], partner).start()

    @pl.when(c == 1)
    def _():
        got(lj.at[0], recv_b.at[0])

    part = dot(lj[0], a_ref[...].astype(BF16), ((1,), (1,)))
    zp[...] = part.reshape(zp.shape)
    for d in far_first(ny):
        there = lax.rem(y + d, ny)
        copy(zp.at[there], zs.at[d], send_y.at[3, d], recv_y.at[3, d], at_y(d)).start()

    @pl.when(row == 0)
    def _():
        total = gpart_ref[y]
        for d in range(1, ny):
            got(gs.at[d], recv_y.at[1, d])
            total += gs[d]
        gr[...] = total
        for d in range(1, nx):
            copy(gr, gx.at[d], send_x.at[1, d], recv_x.at[1, d], at_x(d)).start()
        for d in range(1, nx):
            got(gx.at[d], recv_x.at[1, d])
            total += gx[d]
        g[y] = total
        for d in far_first(ny):
            copy(g.at[y], g.at[y], send_y.at[4, d], recv_y.at[4, d], at_y(d)).start()

    total = zp[y]
    for d in range(1, ny):
        got(zs.at[d], recv_y.at[3, d])
        total += zs[d]
    zr[...] = total
    for d in range(1, nx):
        copy(zr, zx.at[d], send_x.at[2, d], recv_x.at[2, d], at_x(d)).start()
    for d in range(1, nx):
        got(zx.at[d], recv_x.at[2, d])
        total += zx[d]
    zi[y] = total
    for d in far_first(ny):
        copy(zi.at[y], zi.at[y], send_y.at[5, d], recv_y.at[5, d], at_y(d)).start()

    for d in range(1, ny):
        from_y = lax.rem(y + ny - d, ny)
        got(li.at[from_y], recv_y.at[2, d])
    panel = li[...].reshape(li.shape[0] * li.shape[1], li.shape[2]).astype(F32)
    mine = dot(total, panel, ((1,), (1,)), HIGHEST)
    kp[...] = mine
    for d in far_first(nz):
        copy(kp, ks.at[d], send_k.at[d], recv_k.at[d], at_z(d)).start()

    for d in range(1, ny):
        from_y = lax.rem(y + ny - d, ny)
        got(zi.at[from_y], recv_y.at[5, d])

    @pl.when(row == col)
    def _():
        for d in far_first(nz):
            copy(zi, zj, send_z.at[1, d], recv_b.at[1], at_z(d)).start()
        copy(zi, zj, send_c.at[1], recv_b.at[1], partner).start()

    @pl.when(row == 0)
    def _():
        for d in range(1, ny):
            from_y = lax.rem(y + ny - d, ny)
            got(g.at[from_y], recv_y.at[4, d])
        for d in far_first(nz):
            copy(g, g, send_z.at[2, d], recv_b.at[2], at_z(d)).start()
        copy(g, g, send_c.at[2], recv_b.at[2], partner).start()
        for d in far_first(nz):
            copy(colp_ref.at[1], lj.at[1], send_z.at[3, d], recv_b.at[4], at_z(d)).start()
        copy(colp_ref.at[1], lj.at[1], send_c.at[3], recv_b.at[4], partner).start()

    for d in range(1, nz):
        got(ks.at[d], recv_k.at[d])
        mine += ks[d]
    kz[...] = mine
    copy(kz, kc, send_c.at[4], recv_c.at[0], partner).start()
    got(kc, recv_c.at[0])
    kf[...] = mine + kc[...]
    for d in far_first(ny):
        copy(kf, kk.at[y], send_y.at[6, d], recv_y.at[6, d], at_y(d)).start()
    kk[y] = mine + kc[...]

    @pl.when((row != 0) & (c == 0))
    def _():
        got(g, recv_b.at[2])
        copy(g, g, send_c.at[2], recv_b.at[2], partner).start()
        got(lj.at[1], recv_b.at[4])
        copy(lj.at[1], lj.at[1], send_c.at[3], recv_b.at[4], partner).start()

    @pl.when((row != col) & (c == col % 2))
    def _():
        got(zj, recv_b.at[1])
        copy(zj, zj, send_c.at[1], recv_b.at[1], partner).start()

    @pl.when(c == 1)
    def _():
        got(g, recv_b.at[2])
        got(lj.at[1], recv_b.at[4])

    @pl.when(c != col % 2)
    def _():
        got(zj, recv_b.at[1])

    for d in range(1, ny):
        from_y = lax.rem(y + ny - d, ny)
        got(kk.at[from_y], recv_y.at[6, d])

    li_out[...] = li[...]
    lj_out[...] = lj[...]
    zi_out[...] = zi[...]
    g_out[...] = g[...]
    k_out[...] = kk[...]

    @pl.when(row == col)
    def _():
        zj_out[...] = zi[...]

    @pl.when(row != col)
    def _():
        zj_out[...] = zj[...]

    for d in range(1, ny):
        sent(li.at[0], send_y.at[2, d])
        sent(zr, send_y.at[3, d])
        sent(zr, send_y.at[5, d])
        sent(kp, send_y.at[6, d])
    for d in range(1, nx):
        sent(zr, send_x.at[2, d])
    for d in range(1, nz):
        sent(kp, send_k.at[d])
    sent(kp, send_c.at[4])

    @pl.when(x == 0)
    def _():
        for d in range(1, nx):
            sent(li.at[0], send_x.at[0, d])

    @pl.when(col == 0)
    def _():
        for d in range(1, ny):
            sent(li.at[0], send_y.at[0, d])

    @pl.when(row == 0)
    def _():
        for d in range(1, ny):
            sent(gr, send_y.at[1, d])
            sent(gr, send_y.at[4, d])
        for d in range(1, nx):
            sent(gr, send_x.at[1, d])
        for d in range(1, nz):
            sent(lj.at[0], send_z.at[0, d])
            sent(g, send_z.at[2, d])
            sent(lj.at[1], send_z.at[3, d])

    @pl.when(c == 0)
    def _():
        sent(lj.at[0], send_c.at[0])
        sent(g, send_c.at[2])
        sent(lj.at[1], send_c.at[3])

    @pl.when(c == col % 2)
    def _():
        sent(zi, send_c.at[1])

    @pl.when(row == col)
    def _():
        for d in range(1, nz):
            sent(zi, send_z.at[1, d])


def finish(a_ref, li_ref, lj_ref, zi_ref, zj_ref, g_ref, k_ref, out_ref):
    row, col = lax.axis_index("row"), lax.axis_index("col")
    size = a_ref.shape[1]
    rows = lax.broadcasted_iota(jnp.int32, (PW, PW), 0)
    lanes = lax.broadcasted_iota(jnp.int32, (PW, PW), 1)
    gram, cross = g_ref[0:PW, 0:PW], g_ref[0:PW, PW : 2 * PW]
    top, top_right = g_ref[PW : 2 * PW, 0:PW], g_ref[PW : 2 * PW, PW : 2 * PW]

    work = gram
    for i in range(PW):
        scale = work[:, i : i + 1] / work[i : i + 1, i : i + 1]
        work = work - jnp.where(rows[:, :1] > i, scale, 0.0) * work[i : i + 1, :]
    diagonal = jnp.sum(jnp.where(rows == lanes, work, 0.0), axis=1, keepdims=True)
    upper = jnp.where(lanes >= rows, work, 0.0) / jnp.sqrt(diagonal)

    shifted = top + upper
    coupling = dot(shifted, upper, ((0,), (0,)), HIGHEST)
    unit = jnp.where(rows == lanes, 1.0, 0.0).astype(F32)
    work = jnp.concatenate([coupling, unit], axis=1)
    tall = lax.broadcasted_iota(jnp.int32, (PW, 1), 0)
    for i in range(PW):
        pivot = work[i : i + 1, :] / work[i : i + 1, i : i + 1]
        work = jnp.where(tall == i, pivot, work - work[:, i : i + 1] * pivot)
    core = work[:, PW : 2 * PW]

    corner = shifted.astype(BF16)
    change = corner.astype(F32) - top.astype(BF16).astype(F32)
    side = dot(cross, change, ((1,), (0,)), HIGHEST)
    projection = k_ref[:, 0:PW] + side + dot(change, cross, ((0,), (1,)), HIGHEST)
    inner = dot(top_right, change, ((1,), (0,)), HIGHEST)
    projection = projection + dot(change, inner, ((0,), (0,)), HIGHEST)
    middle = dot(core, projection, ((0,), (0,)), HIGHEST)
    middle = dot(middle, core, ((1,), (0,)), HIGHEST)
    corner_t = corner.astype(F32).T

    def pair(left, right, images, first):
        ahead = left[:, 0 : 2 * PW]
        spread = jnp.concatenate([jnp.zeros((PW, PW), F32), corner_t], axis=1)
        wide = lax.broadcasted_iota(jnp.int32, (PW, 2 * PW), 1)
        placed = jnp.where((wide >= PW) & first, spread, ahead.astype(F32))
        basis = jnp.concatenate([placed.astype(BF16), left[:, 2 * PW :]], axis=1)
        full = images + dot(change, right.astype(F32), ((0,), (0,)), HIGHEST)
        update = dot(core, full, ((0,), (0,)), HIGHEST)
        update = update - 0.5 * dot(middle, basis.astype(F32), ((0,), (0,)), HIGHEST)
        return basis, update.astype(BF16)

    basis_i, update_i = pair(li_ref[0], li_ref[1], zi_ref[...], row == 0)
    basis_j, update_j = pair(lj_ref[0], lj_ref[1], zj_ref[...], col == 0)
    left = jnp.concatenate([basis_i, update_i], axis=0)
    right = jnp.concatenate([update_j, basis_j], axis=0)
    for i in range(0, size, 128):
        out_ref[i : i + 128, :] = a_ref[i : i + 128, :] - dot(
            left[:, i : i + 128], right, ((0,), (0,))
        )


def on_device(shape, matrix):
    nz, nx, ny = shape
    size = matrix.shape[0]
    row, col = lax.axis_index("row"), lax.axis_index("col")
    places = jnp.arange(size, dtype=jnp.int32)
    bands = jnp.arange(2 * PW, dtype=jnp.int32)[:, None]
    row_panel = jnp.where(
        (row == 0) & (places < PW)[None, :] & (bands < PW), 0.0, matrix[:, : 2 * PW].T
    )
    col_panel = jnp.where(
        (col == 0) & (places < PW)[None, :] & (bands < PW), 0.0, matrix[: 2 * PW, :]
    )
    left = col_panel[:PW]
    gram = dot(left, left, ((1,), (1,)), HIGHEST)
    half = col_panel.astype(BF16)
    cross = dot(half[:PW], half[PW:], ((1,), (1,)))
    top = jnp.where(col == 0, matrix[PW : 2 * PW, : 2 * PW], 0.0)
    top = jnp.concatenate([top[:, :PW], top[:, PW:].astype(BF16).astype(F32)], axis=1)
    gram_part = jnp.concatenate([jnp.concatenate([gram, cross], axis=1), top], axis=0)

    tall, low = 2 * PW // ny, PW // ny
    vmem = pl.BlockSpec(memory_space=pltpu.VMEM)
    dma = pltpu.SemaphoreType.DMA
    out_shape = (
        jax.ShapeDtypeStruct((ny, tall, size), BF16),
        jax.ShapeDtypeStruct((2, PW, size), BF16),
        jax.ShapeDtypeStruct((ny, low, size), F32),
        jax.ShapeDtypeStruct((ny, low, size), F32),
        jax.ShapeDtypeStruct((ny, tall, 2 * PW), F32),
        jax.ShapeDtypeStruct((ny, low, 2 * PW), F32),
    )
    scratch = [
        pltpu.VMEM((ny, tall, size), BF16),
        pltpu.VMEM((2, PW, size), BF16),
        pltpu.VMEM((ny, low, size), F32),
        pltpu.VMEM((ny, low, size), F32),
        pltpu.VMEM((low, size), F32),
        pltpu.VMEM((nx, low, size), F32),
        pltpu.VMEM((ny, low, size), F32),
        pltpu.VMEM((ny, low, size), F32),
        pltpu.VMEM((ny, tall, 2 * PW), F32),
        pltpu.VMEM((tall, 2 * PW), F32),
        pltpu.VMEM((nx, tall, 2 * PW), F32),
        pltpu.VMEM((ny, tall, 2 * PW), F32),
        pltpu.VMEM((low, 2 * PW), F32),
        pltpu.VMEM((nz, low, 2 * PW), F32),
        pltpu.VMEM((low, 2 * PW), F32),
        pltpu.VMEM((low, 2 * PW), F32),
        pltpu.VMEM((low, 2 * PW), F32),
        pltpu.VMEM((ny, low, 2 * PW), F32),
        dma((4, nz)), dma((1,)), dma((7, ny)), dma((7, ny)), dma((3, nx)), dma((3, nx)),
        dma((nz,)), dma((nz,)), dma((1,)), dma((5,)), dma((5,)), dma((1,)),
    ]
    li, lj, zi, zj, g, k = pl.pallas_call(
        functools.partial(exchange, shape),
        out_shape=out_shape,
        in_specs=[vmem] * 4,
        out_specs=(vmem,) * 6,
        scratch_shapes=scratch,
        compiler_params=pltpu.CompilerParams(collective_id=0, has_side_effects=True),
        name="exchange",
    )(
        matrix,
        row_panel.astype(BF16).reshape(ny, tall, size),
        half.reshape(2, PW, size),
        gram_part.reshape(ny, tall, 2 * PW),
    )
    return pl.pallas_call(
        finish,
        out_shape=jax.ShapeDtypeStruct(matrix.shape, F32),
        in_specs=[vmem] * 7,
        out_specs=vmem,
        name="finish",
    )(
        matrix,
        li.reshape(2, PW, size),
        lj,
        zi.reshape(PW, size),
        zj.reshape(PW, size),
        g.reshape(2 * PW, 2 * PW),
        k.reshape(PW, 2 * PW),
    )


def grid_of(mesh):
    rows, cols = mesh.shape["row"], mesh.shape["col"]
    return {(32, 32): (16, 4, 8), (4, 4): (2, 2, 2)}[(rows, cols)]


def solution(mesh):
    return jax.shard_map(
        functools.partial(on_device, grid_of(mesh)),
        mesh=mesh,
        in_specs=(P("row", "col"),),
        out_specs=P("row", "col"),
        check_vma=False,
    )
```

time: 909 us -> 99.7 us (0.11)
  the two profiles are of different devices: /device:TPU:2 before, /device:TPU:65 now
where the time goes in v1:
time: 99.7 us; the launch traced here: 99.4 us
  Pallas kernels  94.3 us (95%)
  other arithmetic  3.46 us (3%)
  local copies, waits for them, and re-layouts  1.16 us (1%)
    pallas_call x1, Pallas kernels, on_device(): pl.pallas_call(functools.partial(exchange, shape), out_shape=out_shape, i...  78.7 us
    pallas_call x1, Pallas kernels, on_device(): pl.pallas_call(finish, out_shape=jax.ShapeDtypeStruct(matrix.shape, F32),...  15.6 us

profile of v1, /device:TPU:65, one launch (start us, length us, event | category | flops | bytes accessed | tf_op | source)
XLA Modules:
  0.0 99.4 jit_solution(17825374232434073675)
XLA Ops:
  0.0 0.8 slice_select_fusion.1
  0.8 0.1 fusion.6
  0.9 1.0 slice.25
  1.9 0.2 copy.3
  2.0 0.8 fusion
  2.8 1.1 %fusion.9 = (bf16[128,640]{1,0:T(8,128)(2,1)S(1)}, f32[128,640]{1,0:T(8,128)S(1)}) fusion(f32[640,640]{1,0:T(8,128)} %a_ref.3, pred[128]{0:T(512)(128)(4,1)S(1)} %iota_compare_fusion.1, pred[640]{0:T(1024)(128)(4,1)S(1)} %fusion.7), kind=kLoop, calls=%fused_computation.16 | loop fusion | flops 245760 | bytes 819968 | tf_op jit(solution)/shard_map/convert_element_type | solution.py:352
  3.9 0.0 copy-start
  3.9 0.3 fusion.1
  4.2 0.1 fusion.3
  4.4 0.7 maximum_maximum_fusion
  5.1 0.0 copy-done
  5.1 78.7 %exchange.1 = (bf16[8,16,640]{2,1,0:T(8,128)(2,1)}, bf16[2,64,640]{2,1,0:T(8,128)(2,1)}, f32[8,8,640]{2,1,0:T(8,128)}, f32[8,8,640]{2,1,0:T(8,128)}, f32[8,16,128]{2,1,0:T(8,128)}, /*index=5*/f32[8,8,128]{2,1,0:T(8,128)}) custom-call(f32[640,640]{1,0:T(8,128)} %a_ref.3, bf16[8,16,640]{2,1,0:T(8,128)(2,1)} %bitcast.13, bf16[2,64,640]{2,1,0:T(8,128)(2,1)} %bitcast.14, ...), custom_call_target="tpu_custom_call" | custom-call | tf_op jit(solution)/shard_map/exchange/pallas_call | solution.py:391
  83.8 15.6 %finish.1 = f32[640,640]{1,0:T(8,128)} custom-call(f32[640,640]{1,0:T(8,128)} %a_ref.3, bf16[2,64,640]{2,1,0:T(8,128)(2,1)} %bitcast.17, bf16[2,64,640]{2,1,0:T(8,128)(2,1)} %get-tuple-element.12.lj_ref, f32[64,640]{1,0:T(8,128)} %bitcast.18, f32[64,640]{1,0:T(8,128)} %bitcast.19, f32[128,128]{1,0:T(8,128)} %bitcast.20, f32[64,128]{1,0:T(8,128)} %bitcast.21), custom_call_target="tpu_custom_call" | custom-call | tf_op jit(solution)/shard_map/finish/pallas_call | solution.py:405
  (3 shorter events, 0.0 us)
Async XLA Ops:
  3.9 1.2 %copy-start = (bf16[128,640]{1,0:T(8,128)(2,1)}, bf16[128,640]{1,0:T(8,128)(2,1)S(1)}, u32[]{:S(2)}) copy-start(bf16[128,640]{1,0:T(8,128)(2,1)S(1)} %get-tuple-element.17) | copy-start | bytes 491524

commit v2 on v1

v2 whole, which is shorter than its diff:
```python
import functools

import jax
import jax.numpy as jnp
from jax import lax
from jax.experimental import pallas as pl
from jax.experimental.pallas import tpu as pltpu
from jax.sharding import PartitionSpec as P

PW = 64
HIGHEST = lax.Precision.HIGHEST
MESH = pl.DeviceIdType.MESH
F32 = jnp.float32
BF16 = jnp.bfloat16


def dot(first, second, dims, precision=None):
    return lax.dot_general(
        first, second, (dims, ((), ())), precision=precision, preferred_element_type=F32
    )


def far_first(count):
    return sorted(range(1, count), key=lambda d: -min(d, count - d))


def eliminate(gram):
    rows = lax.broadcasted_iota(jnp.int32, (PW, PW), 0)
    lanes = lax.broadcasted_iota(jnp.int32, (PW, PW), 1)
    work = gram
    for i in range(PW):
        scale = work[:, i : i + 1] / work[i : i + 1, i : i + 1]
        work = work - jnp.where(rows[:, :1] > i, scale, 0.0) * work[i : i + 1, :]
    diagonal = jnp.sum(jnp.where(rows == lanes, work, 0.0), axis=1, keepdims=True)
    return jnp.where(lanes >= rows, work, 0.0) / jnp.sqrt(diagonal)


def invert(coupling):
    rows = lax.broadcasted_iota(jnp.int32, (PW, PW), 0)
    lanes = lax.broadcasted_iota(jnp.int32, (PW, PW), 1)
    tall = lax.broadcasted_iota(jnp.int32, (PW, 1), 0)
    unit = jnp.where(rows == lanes, 1.0, 0.0).astype(F32)
    work = jnp.concatenate([coupling, unit], axis=1)
    for i in range(PW):
        pivot = work[i : i + 1, :] / work[i : i + 1, i : i + 1]
        work = jnp.where(tall == i, pivot, work - work[:, i : i + 1] * pivot)
    return work[:, PW : 2 * PW]


def basis_of(left, corner_t, first):
    spread = jnp.concatenate([jnp.zeros((PW, PW), F32), corner_t], axis=1)
    wide = lax.broadcasted_iota(jnp.int32, (PW, 2 * PW), 1)
    placed = jnp.where((wide >= PW) & first, spread, left[:, : 2 * PW].astype(F32))
    return jnp.concatenate([placed.astype(BF16), left[:, 2 * PW :]], axis=1)


def exchange(shape, a_hbm, left_out, right_out,
             a, rowp, colp, gpart,
             li, lj, zp, zs, zr, zx, zi, zj, gs, gr, gx, g, kp, ks, kz, kc, kf, kk,
             upper_ref, core_ref,
             a_sem, send_z, send_d, send_y, recv_y, send_x, recv_x, send_k, recv_k,
             recv_b, recv_d, send_c, recv_c):
    nz, nx, ny = shape
    size = a.shape[0]
    row, col = lax.axis_index("row"), lax.axis_index("col")
    z, c = row // 2, row % 2
    x, y = col // ny, col % ny
    partner = (z * 2 + 1 - c, col)

    def at_z(d):
        return (lax.rem(z + d, nz) * 2 + c, col)

    def at_y(d):
        return (row, x * ny + lax.rem(y + d, ny))

    def at_x(d):
        return (row, lax.rem(x + d, nx) * ny + y)

    def to_y(d):
        return lax.rem(y + d, ny)

    def from_y(d):
        return lax.rem(y + ny - d, ny)

    def copy(src, dst, send, recv, where):
        return pltpu.make_async_remote_copy(
            src_ref=src, dst_ref=dst, send_sem=send, recv_sem=recv,
            device_id=where, device_id_type=MESH,
        )

    def got(ref, sem):
        copy(ref, ref, sem, sem, partner).wait_recv()

    def sent(ref, sem):
        copy(ref, ref, sem, sem, partner).wait_send()

    fetch = pltpu.make_async_copy(a_hbm, a, a_sem.at[0])
    fetch.start()
    barrier = pltpu.get_barrier_semaphore()
    peers = [at_z(d) for d in range(1, nz)] + [at_y(d) for d in range(1, ny)]
    peers += [at_x(d) for d in range(1, nx)] + [partner]
    for peer in peers:
        pl.semaphore_signal(barrier, inc=1, device_id=peer, device_id_type=MESH)
    fetch.wait()

    bands = lax.broadcasted_iota(jnp.int32, (2 * PW, size), 0)
    places = lax.broadcasted_iota(jnp.int32, (2 * PW, size), 1)
    hidden = (bands < PW) & (places < PW)

    @pl.when(col == 0)
    def _():
        panel = jnp.where(hidden & (row == 0), 0.0, a[:, : 2 * PW].T)
        rowp[...] = panel.astype(BF16).reshape(rowp.shape)

    @pl.when(row == 0)
    def _():
        panel = jnp.where(hidden & (col == 0), 0.0, a[: 2 * PW, :])
        half = panel.astype(BF16)
        colp[...] = half.reshape(colp.shape)
        lj[...] = half.reshape(colp.shape)
        gram = dot(panel[:PW], panel[:PW], ((1,), (1,)), HIGHEST)
        cross = dot(half[:PW], half[PW:], ((1,), (1,)))
        right = a[PW : 2 * PW, PW : 2 * PW].astype(BF16).astype(F32)
        top = jnp.concatenate([a[PW : 2 * PW, :PW], right], axis=1)
        top = jnp.where(col == 0, top, 0.0)
        whole = jnp.concatenate([jnp.concatenate([gram, cross], axis=1), top], axis=0)
        gpart[...] = whole.reshape(gpart.shape)

    pl.semaphore_wait(barrier, len(peers))

    @pl.when(row == 0)
    def _():
        for d in far_first(nz):
            copy(colp.at[0], lj.at[0], send_z.at[0, d], recv_b.at[0], at_z(d)).start()
        copy(colp.at[0], lj.at[0], send_c.at[0], recv_b.at[0], partner).start()
        for d in far_first(ny):
            copy(gpart.at[to_y(d)], gs.at[d], send_y.at[1, d], recv_y.at[1, d], at_y(d)).start()

    @pl.when(col == 0)
    def _():
        for d in far_first(ny):
            copy(rowp.at[d], li.at[d], send_y.at[0, d], recv_b.at[2], at_y(d)).start()
        for d in range(1, nx):
            copy(rowp.at[0], li.at[0], send_x.at[0, d], recv_x.at[0, 0], at_x(d)).start()
        li[0] = rowp[0]

    @pl.when(row == 0)
    def _():
        total = gpart[y]
        for d in range(1, ny):
            got(gs.at[d], recv_y.at[1, d])
            total += gs[d]
        gr[...] = total
        for d in range(1, nx):
            copy(gr, gx.at[d], send_x.at[1, d], recv_x.at[1, d], at_x(d)).start()

    @pl.when((x == 0) & (y != 0))
    def _():
        got(li.at[y], recv_b.at[2])
        for d in range(1, nx):
            copy(li.at[y], li.at[y], send_x.at[0, d], recv_x.at[0, 0], at_x(d)).start()

    @pl.when(row == 0)
    def _():
        total = gr[...]
        for d in range(1, nx):
            got(gx.at[d], recv_x.at[1, d])
            total += gx[d]
        g[y] = total
        for d in far_first(ny):
            copy(g.at[y], g.at[y], send_y.at[4, d], recv_y.at[4, d], at_y(d)).start()

    @pl.when(x != 0)
    def _():
        got(li.at[y], recv_x.at[0, 0])

    @pl.when(col == 0)
    def _():
        for d in far_first(ny):
            copy(rowp.at[0], li.at[0], send_y.at[2, d], recv_y.at[2, d], at_y(d)).start()

    @pl.when(col != 0)
    def _():
        for d in far_first(ny):
            copy(li.at[y], li.at[y], send_y.at[2, d], recv_y.at[2, d], at_y(d)).start()

    @pl.when((row != 0) & (c == 0))
    def _():
        got(lj.at[0], recv_b.at[0])
        copy(lj.at[0], lj.at[0], send_c.at[0], recv_b.at[0], partner).start()

    @pl.when(c == 1)
    def _():
        got(lj.at[0], recv_b.at[0])

    part = dot(lj[0], a[...].astype(BF16), ((1,), (1,)))
    zp[...] = part.reshape(zp.shape)
    for d in far_first(ny):
        copy(zp.at[to_y(d)], zs.at[d], send_y.at[3, d], recv_y.at[3, d], at_y(d)).start()

    @pl.when(row == 0)
    def _():
        for d in range(1, ny):
            got(g.at[from_y(d)], recv_y.at[4, d])
        for d in far_first(nz):
            copy(g, g, send_z.at[1, d], recv_b.at[1], at_z(d)).start()
        copy(g, g, send_c.at[1], recv_b.at[1], partner).start()
        for d in far_first(nz):
            copy(colp.at[1], lj.at[1], send_z.at[2, d], recv_b.at[3], at_z(d)).start()
        copy(colp.at[1], lj.at[1], send_c.at[2], recv_b.at[3], partner).start()

    total = zp[y]
    for d in range(1, ny):
        got(zs.at[d], recv_y.at[3, d])
        total += zs[d]
    zr[...] = total
    for d in range(1, nx):
        copy(zr, zx.at[d], send_x.at[2, d], recv_x.at[2, d], at_x(d)).start()

    for d in range(1, ny):
        got(li.at[from_y(d)], recv_y.at[2, d])
    panel = li[...].reshape(2 * PW, size)

    for d in range(1, nx):
        got(zx.at[d], recv_x.at[2, d])
        total += zx[d]
    zi[y] = total
    for d in far_first(ny):
        copy(zi.at[y], zi.at[y], send_y.at[5, d], recv_y.at[5, d], at_y(d)).start()

    mine = dot(total, panel.astype(F32), ((1,), (1,)), HIGHEST)
    kp[...] = mine
    for d in far_first(nz):
        copy(kp, ks.at[d], send_k.at[d], recv_k.at[d], at_z(d)).start()

    def forward(d):
        @pl.when(row == col)
        def _():
            there = from_y(d)
            for e in far_first(nz):
                copy(zi.at[there], zj.at[there], send_d.at[d, e], recv_d.at[there], at_z(e)).start()
            copy(zi.at[there], zj.at[there], send_d.at[d, 0], recv_d.at[there], partner).start()

    forward(0)

    @pl.when((row != 0) & (c == 0))
    def _():
        got(g, recv_b.at[1])
        copy(g, g, send_c.at[1], recv_b.at[1], partner).start()

    @pl.when(c == 1)
    def _():
        got(g, recv_b.at[1])

    whole = g[...].reshape(2 * PW, 2 * PW)
    gram, cross = whole[:PW, :PW], whole[:PW, PW:]
    top, top_right = whole[PW:, :PW], whole[PW:, PW:]
    upper_ref[...] = eliminate(gram)

    for d in range(1, ny):
        got(zi.at[from_y(d)], recv_y.at[5, d])
        forward(d)

    for d in range(1, nz):
        got(ks.at[d], recv_k.at[d])
        mine += ks[d]
    kz[...] = mine
    copy(kz, kc, send_c.at[3], recv_c.at[0], partner).start()

    upper = upper_ref[...]
    shifted = top + upper
    core_ref[...] = invert(dot(shifted, upper, ((0,), (0,)), HIGHEST))
    core = core_ref[...]

    got(kc, recv_c.at[0])
    mine += kc[...]
    kf[...] = mine
    for d in far_first(ny):
        copy(kf, kk.at[y], send_y.at[6, d], recv_y.at[6, d], at_y(d)).start()
    kk[y] = mine

    @pl.when((row != 0) & (c == 0))
    def _():
        got(lj.at[1], recv_b.at[3])
        copy(lj.at[1], lj.at[1], send_c.at[2], recv_b.at[3], partner).start()

    corner = shifted.astype(BF16)
    change = corner.astype(F32) - top.astype(BF16).astype(F32)
    corner_t = corner.astype(F32).T
    side = dot(cross, change, ((1,), (0,)), HIGHEST)
    side = side + dot(change, cross, ((0,), (1,)), HIGHEST)
    inner = dot(top_right, change, ((1,), (0,)), HIGHEST)
    side = side + dot(change, inner, ((0,), (0,)), HIGHEST)

    def first_term(right, images):
        full = images + dot(change, right.astype(F32), ((0,), (0,)), HIGHEST)
        return dot(core, full, ((0,), (0,)), HIGHEST)

    basis_i = basis_of(panel[:PW], corner_t, row == 0)
    basis_j = basis_of(lj[0], corner_t, col == 0)
    left_out[:PW, :] = basis_i
    right_out[PW:, :] = basis_j
    first_i = first_term(panel[PW:], zi[...].reshape(PW, size))

    @pl.when((row != col) & (c == col % 2))
    def _():
        for d in range(ny):
            there = d
            got(zj.at[there], recv_d.at[there])
            copy(zj.at[there], zj.at[there], send_d.at[d, 0], recv_d.at[there], partner).start()

    @pl.when(c != col % 2)
    def _():
        for d in range(ny):
            got(zj.at[d], recv_d.at[d])

    @pl.when(c == 1)
    def _():
        got(lj.at[1], recv_b.at[3])

    @pl.when(row == col)
    def _():
        zj[...] = zi[...]

    first_j = first_term(lj[1], zj[...].reshape(PW, size))

    for d in range(1, ny):
        got(kk.at[from_y(d)], recv_y.at[6, d])
    projection = kk[...].reshape(PW, 2 * PW)[:, :PW] + side
    middle = dot(core, projection, ((0,), (0,)), HIGHEST)
    middle = dot(middle, core, ((1,), (0,)), HIGHEST)

    def update_of(first, basis):
        second = dot(middle, basis.astype(F32), ((0,), (0,)), HIGHEST)
        return (first - 0.5 * second).astype(BF16)

    left_out[PW:, :] = update_of(first_i, basis_i)
    right_out[:PW, :] = update_of(first_j, basis_j)

    for d in range(1, ny):
        sent(li.at[0], send_y.at[2, d])
        sent(zr, send_y.at[3, d])
        sent(zr, send_y.at[5, d])
        sent(kp, send_y.at[6, d])
    for d in range(1, nx):
        sent(zr, send_x.at[2, d])
    for d in range(1, nz):
        sent(kp, send_k.at[d])
    sent(kp, send_c.at[3])

    @pl.when(x == 0)
    def _():
        for d in range(1, nx):
            sent(li.at[0], send_x.at[0, d])

    @pl.when(col == 0)
    def _():
        for d in range(1, ny):
            sent(li.at[0], send_y.at[0, d])

    @pl.when(row == 0)
    def _():
        for d in range(1, ny):
            sent(gr, send_y.at[1, d])
            sent(gr, send_y.at[4, d])
        for d in range(1, nx):
            sent(gr, send_x.at[1, d])
        for d in range(1, nz):
            sent(lj.at[0], send_z.at[0, d])
            sent(g, send_z.at[1, d])
            sent(lj.at[1], send_z.at[2, d])

    @pl.when(c == 0)
    def _():
        sent(lj.at[0], send_c.at[0])
        sent(g, send_c.at[1])
        sent(lj.at[1], send_c.at[2])

    @pl.when(c == col % 2)
    def _():
        for d in range(ny):
            sent(zr, send_d.at[d, 0])

    @pl.when(row == col)
    def _():
        for d in range(ny):
            for e in range(1, nz):
                sent(zr, send_d.at[d, e])


def on_device(shape, matrix):
    nz, nx, ny = shape
    size = matrix.shape[0]
    tall, low = 2 * PW // ny, PW // ny
    dma = pltpu.SemaphoreType.DMA
    scratch = [
        pltpu.VMEM((size, size), F32),
        pltpu.VMEM((ny, tall, size), BF16),
        pltpu.VMEM((2, PW, size), BF16),
        pltpu.VMEM((ny, tall, 2 * PW), F32),
        pltpu.VMEM((ny, tall, size), BF16),
        pltpu.VMEM((2, PW, size), BF16),
        pltpu.VMEM((ny, low, size), F32),
        pltpu.VMEM((ny, low, size), F32),
        pltpu.VMEM((low, size), F32),
        pltpu.VMEM((nx, low, size), F32),
        pltpu.VMEM((ny, low, size), F32),
        pltpu.VMEM((ny, low, size), F32),
        pltpu.VMEM((ny, tall, 2 * PW), F32),
        pltpu.VMEM((tall, 2 * PW), F32),
        pltpu.VMEM((nx, tall, 2 * PW), F32),
        pltpu.VMEM((ny, tall, 2 * PW), F32),
        pltpu.VMEM((low, 2 * PW), F32),
        pltpu.VMEM((nz, low, 2 * PW), F32),
        pltpu.VMEM((low, 2 * PW), F32),
        pltpu.VMEM((low, 2 * PW), F32),
        pltpu.VMEM((low, 2 * PW), F32),
        pltpu.VMEM((ny, low, 2 * PW), F32),
        pltpu.VMEM((PW, PW), F32),
        pltpu.VMEM((PW, PW), F32),
        dma((1,)), dma((3, nz)), dma((ny, nz)), dma((7, ny)), dma((7, ny)),
        dma((3, nx)), dma((3, nx)), dma((nz,)), dma((nz,)),
        dma((4,)), dma((ny,)), dma((4,)), dma((1,)),
    ]
    vmem = pl.BlockSpec(memory_space=pltpu.VMEM)
    left, right = pl.pallas_call(
        functools.partial(exchange, shape),
        out_shape=(jax.ShapeDtypeStruct((2 * PW, size), BF16),) * 2,
        in_specs=[pl.BlockSpec(memory_space=pl.ANY)],
        out_specs=(vmem, vmem),
        scratch_shapes=scratch,
        compiler_params=pltpu.CompilerParams(collective_id=0, has_side_effects=True),
        name="exchange",
    )(matrix)
    return matrix - dot(left, right, ((0,), (0,)))


def grid_of(mesh):
    rows, cols = mesh.shape["row"], mesh.shape["col"]
    return {(32, 32): (16, 4, 8), (4, 4): (2, 2, 2)}[(rows, cols)]


def solution(mesh):
    return jax.shard_map(
        functools.partial(on_device, grid_of(mesh)),
        mesh=mesh,
        in_specs=(P("row", "col"),),
        out_specs=P("row", "col"),
        check_vma=False,
    )
```

time: 99.7 us -> 77.7 us (0.78)
  the two profiles are of different devices: /device:TPU:65 before, /device:TPU:70 now
where the time goes in v2:
time: 77.7 us; the launch traced here: 77.5 us
  Pallas kernels  74.9 us (96%)
  matrix products  2.56 us (3%)
    pallas_call x1, Pallas kernels, on_device(): pl.pallas_call(functools.partial(exchange, shape), out_shape=(jax.ShapeDt...  74.9 us
    dot_general x1, matrix products, dot(): lax.dot_general(first, second, (dims, ((), ())), precision=precision, pre...  2.56 us

profile of v2, /device:TPU:70, one launch (start us, length us, event | category | flops | bytes accessed | tf_op | source)
XLA Modules:
  0.0 77.5 jit_solution(17433432310860679244)
XLA Ops:
  0.0 0.0 copy-start
  0.0 74.9 %exchange.1 = (bf16[128,640]{1,0:T(8,128)(2,1)}, bf16[128,640]{1,0:T(8,128)(2,1)}) custom-call(f32[640,640]{1,0:T(8,128)} %a_hbm.1), custom_call_target="tpu_custom_call" | custom-call | tf_op jit(solution)/shard_map/exchange/pallas_call | solution.py:426
  74.9 0.0 copy-done
  74.9 2.6 %convolution_subtract_fusion = f32[640,640]{1,0:T(8,128)} fusion(f32[640,640]{1,0:T(8,128)S(1)} %copy-done, bf16[128,640]{1,0:T(8,128)(2,1)} %get-tuple-element.7, bf16[128,640]{1,0:T(8,128)(2,1)} %get-tuple-element.8), kind=kOutput, calls=%fused_computation | convolution fusion | flops 105267200 | bytes 3604480 | tf_op jit(solution)/shard_map/dot_general | solution.py:18
Async XLA Ops:
  0.0 74.9 %copy-start = (f32[640,640]{1,0:T(8,128)S(1)}, f32[640,640]{1,0:T(8,128)}, u32[]{:S(2)}) copy-start(f32[640,640]{1,0:T(8,128)} %a_hbm.1) | copy-start | bytes 4915204

commit v3 on v2

--- a/solution.py
+++ b/solution.py
@@ -27,12 +27,15 @@
 def eliminate(gram):
     rows = lax.broadcasted_iota(jnp.int32, (PW, PW), 0)
     lanes = lax.broadcasted_iota(jnp.int32, (PW, PW), 1)
-    work = gram
+    unit = jnp.where(rows == lanes, 1.0, 0.0).astype(F32)
+    work = jnp.concatenate([gram, unit], axis=1)
     for i in range(PW):
         scale = work[:, i : i + 1] / work[i : i + 1, i : i + 1]
         work = work - jnp.where(rows[:, :1] > i, scale, 0.0) * work[i : i + 1, :]
-    diagonal = jnp.sum(jnp.where(rows == lanes, work, 0.0), axis=1, keepdims=True)
-    return jnp.where(lanes >= rows, work, 0.0) / jnp.sqrt(diagonal)
+    upper, lower = work[:, :PW], work[:, PW:]
+    diagonal = jnp.sum(jnp.where(rows == lanes, upper, 0.0), axis=1, keepdims=True)
+    root = jnp.sqrt(diagonal)
+    return jnp.where(lanes >= rows, upper, 0.0) / root, jnp.where(lanes <= rows, lower, 0.0) / root
 
 
 def invert(coupling):
@@ -56,10 +59,9 @@
 
 def exchange(shape, a_hbm, left_out, right_out,
              a, rowp, colp, gpart,
-             li, lj, zp, zs, zr, zx, zi, zj, gs, gr, gx, g, kp, ks, kz, kc, kf, kk,
-             upper_ref, core_ref,
+             li, lj, zp, zs, zr, zx, zi, zh, zj, gs, gr, gx, g, kp, ks, kz, kc, kf, kk,
              a_sem, send_z, send_d, send_y, recv_y, send_x, recv_x, send_k, recv_k,
-             recv_b, recv_d, send_c, recv_c):
+             recv_b, send_c, recv_c):
     nz, nx, ny = shape
     size = a.shape[0]
     row, col = lax.axis_index("row"), lax.axis_index("col")
@@ -233,16 +235,6 @@
     for d in far_first(nz):
         copy(kp, ks.at[d], send_k.at[d], recv_k.at[d], at_z(d)).start()
 
-    def forward(d):
-        @pl.when(row == col)
-        def _():
-            there = from_y(d)
-            for e in far_first(nz):
-                copy(zi.at[there], zj.at[there], send_d.at[d, e], recv_d.at[there], at_z(e)).start()
-            copy(zi.at[there], zj.at[there], send_d.at[d, 0], recv_d.at[there], partner).start()
-
-    forward(0)
-
     @pl.when((row != 0) & (c == 0))
     def _():
         got(g, recv_b.at[1])
@@ -255,11 +247,20 @@
     whole = g[...].reshape(2 * PW, 2 * PW)
     gram, cross = whole[:PW, :PW], whole[:PW, PW:]
     top, top_right = whole[PW:, :PW], whole[PW:, PW:]
-    upper_ref[...] = eliminate(gram)
+    upper, inverse_t = eliminate(gram)
 
     for d in range(1, ny):
         got(zi.at[from_y(d)], recv_y.at[5, d])
-        forward(d)
+    images = zi[...].reshape(PW, size)
+
+    @pl.when(row == col)
+    def _():
+        half = dot(inverse_t, images, ((1,), (0,)), HIGHEST).astype(BF16)
+        zh[...] = half
+        zj[...] = half
+        for d in far_first(nz):
+            copy(zh, zj, send_d.at[d], recv_b.at[4], at_z(d)).start()
+        copy(zh, zj, send_d.at[0], recv_b.at[4], partner).start()
 
     for d in range(1, nz):
         got(ks.at[d], recv_k.at[d])
@@ -267,10 +268,14 @@
     kz[...] = mine
     copy(kz, kc, send_c.at[3], recv_c.at[0], partner).start()
 
-    upper = upper_ref[...]
     shifted = top + upper
-    core_ref[...] = invert(dot(shifted, upper, ((0,), (0,)), HIGHEST))
-    core = core_ref[...]
+    coupling = dot(shifted, upper, ((0,), (0,)), HIGHEST)
+    corner = shifted.astype(BF16)
+    change = corner.astype(F32) - top.astype(BF16).astype(F32)
+    side = dot(cross, change, ((1,), (0,)), HIGHEST)
+    side = side + dot(change, cross, ((0,), (1,)), HIGHEST)
+    inner = dot(top_right, change, ((1,), (0,)), HIGHEST)
+    side = side + dot(change, inner, ((0,), (0,)), HIGHEST)
 
     got(kc, recv_c.at[0])
     mine += kc[...]
@@ -284,58 +289,42 @@
         got(lj.at[1], recv_b.at[3])
         copy(lj.at[1], lj.at[1], send_c.at[2], recv_b.at[3], partner).start()
 
-    corner = shifted.astype(BF16)
-    change = corner.astype(F32) - top.astype(BF16).astype(F32)
+    @pl.when(c == 1)
+    def _():
+        got(lj.at[1], recv_b.at[3])
+
+    core = invert(coupling)
     corner_t = corner.astype(F32).T
-    side = dot(cross, change, ((1,), (0,)), HIGHEST)
-    side = side + dot(change, cross, ((0,), (1,)), HIGHEST)
-    inner = dot(top_right, change, ((1,), (0,)), HIGHEST)
-    side = side + dot(change, inner, ((0,), (0,)), HIGHEST)
-
-    def first_term(right, images):
-        full = images + dot(change, right.astype(F32), ((0,), (0,)), HIGHEST)
-        return dot(core, full, ((0,), (0,)), HIGHEST)
-
-    basis_i = basis_of(panel[:PW], corner_t, row == 0)
+    basis_i = basis_of(panel[:PW], corner_t, row == 0).astype(F32).T
     basis_j = basis_of(lj[0], corner_t, col == 0)
-    left_out[:PW, :] = basis_i
     right_out[PW:, :] = basis_j
-    first_i = first_term(panel[PW:], zi[...].reshape(PW, size))
-
-    @pl.when((row != col) & (c == col % 2))
-    def _():
-        for d in range(ny):
-            there = d
-            got(zj.at[there], recv_d.at[there])
-            copy(zj.at[there], zj.at[there], send_d.at[d, 0], recv_d.at[there], partner).start()
-
-    @pl.when(c != col % 2)
-    def _():
-        for d in range(ny):
-            got(zj.at[d], recv_d.at[d])
-
-    @pl.when(c == 1)
-    def _():
-        got(lj.at[1], recv_b.at[3])
-
-    @pl.when(row == col)
-    def _():
-        zj[...] = zi[...]
-
-    first_j = first_term(lj[1], zj[...].reshape(PW, size))
+    shift = dot(change, core, ((1,), (0,)), HIGHEST)
+    first_i = dot(core, images, ((0,), (0,)), HIGHEST)
+    first_i = first_i + dot(shift, panel[PW:].astype(F32), ((0,), (0,)), HIGHEST)
+    first_i = first_i.T
+    shift_j = dot(shift, lj[1].astype(F32), ((0,), (0,)), HIGHEST)
+    scaled = dot(upper, core, ((1,), (0,)), HIGHEST)
 
     for d in range(1, ny):
         got(kk.at[from_y(d)], recv_y.at[6, d])
     projection = kk[...].reshape(PW, 2 * PW)[:, :PW] + side
     middle = dot(core, projection, ((0,), (0,)), HIGHEST)
-    middle = dot(middle, core, ((1,), (0,)), HIGHEST)
-
-    def update_of(first, basis):
-        second = dot(middle, basis.astype(F32), ((0,), (0,)), HIGHEST)
-        return (first - 0.5 * second).astype(BF16)
-
-    left_out[PW:, :] = update_of(first_i, basis_i)
-    right_out[:PW, :] = update_of(first_j, basis_j)
+    middle = 0.5 * dot(middle, core, ((1,), (0,)), HIGHEST)
+    update_i = first_i - dot(basis_i, middle, ((1,), (0,)), HIGHEST)
+    left_out[...] = jnp.concatenate([basis_i, update_i], axis=1).astype(BF16)
+    shift_j = shift_j - dot(middle, basis_j.astype(F32), ((0,), (0,)), HIGHEST)
+
+    @pl.when((row != col) & (c == col % 2))
+    def _():
+        got(zj, recv_b.at[4])
+        copy(zj, zj, send_d.at[0], recv_b.at[4], partner).start()
+
+    @pl.when(c != col % 2)
+    def _():
+        got(zj, recv_b.at[4])
+
+    first_j = dot(scaled, zj[...].astype(F32), ((0,), (0,)), HIGHEST)
+    right_out[:PW, :] = (first_j + shift_j).astype(BF16)
 
     for d in range(1, ny):
         sent(li.at[0], send_y.at[2, d])
@@ -378,14 +367,12 @@
 
     @pl.when(c == col % 2)
     def _():
-        for d in range(ny):
-            sent(zr, send_d.at[d, 0])
+        sent(zh, send_d.at[0])
 
     @pl.when(row == col)
     def _():
-        for d in range(ny):
-            for e in range(1, nz):
-                sent(zr, send_d.at[d, e])
+        for d in range(1, nz):
+            sent(zh, send_d.at[d])
 
 
 def on_device(shape, matrix):
@@ -405,7 +392,8 @@
         pltpu.VMEM((low, size), F32),
         pltpu.VMEM((nx, low, size), F32),
         pltpu.VMEM((ny, low, size), F32),
-        pltpu.VMEM((ny, low, size), F32),
+        pltpu.VMEM((PW, size), BF16),
+        pltpu.VMEM((PW, size), BF16),
         pltpu.VMEM((ny, tall, 2 * PW), F32),
         pltpu.VMEM((tall, 2 * PW), F32),
         pltpu.VMEM((nx, tall, 2 * PW), F32),
@@ -416,23 +404,24 @@
         pltpu.VMEM((low, 2 * PW), F32),
         pltpu.VMEM((low, 2 * PW), F32),
         pltpu.VMEM((ny, low, 2 * PW), F32),
-        pltpu.VMEM((PW, PW), F32),
-        pltpu.VMEM((PW, PW), F32),
-        dma((1,)), dma((3, nz)), dma((ny, nz)), dma((7, ny)), dma((7, ny)),
+        dma((1,)), dma((3, nz)), dma((nz,)), dma((7, ny)), dma((7, ny)),
         dma((3, nx)), dma((3, nx)), dma((nz,)), dma((nz,)),
-        dma((4,)), dma((ny,)), dma((4,)), dma((1,)),
+        dma((5,)), dma((4,)), dma((1,)),
     ]
     vmem = pl.BlockSpec(memory_space=pltpu.VMEM)
     left, right = pl.pallas_call(
         functools.partial(exchange, shape),
-        out_shape=(jax.ShapeDtypeStruct((2 * PW, size), BF16),) * 2,
+        out_shape=(
+            jax.ShapeDtypeStruct((size, 2 * PW), BF16),
+            jax.ShapeDtypeStruct((2 * PW, size), BF16),
+        ),
         in_specs=[pl.BlockSpec(memory_space=pl.ANY)],
         out_specs=(vmem, vmem),
         scratch_shapes=scratch,
         compiler_params=pltpu.CompilerParams(collective_id=0, has_side_effects=True),
         name="exchange",
     )(matrix)
-    return matrix - dot(left, right, ((0,), (0,)))
+    return matrix - dot(left, right, ((1,), (0,)))
 
 
 def grid_of(mesh):

time: 77.7 us -> 72.7 us (0.936)
  the two profiles are of different devices: /device:TPU:70 before, /device:TPU:72 now
where the time goes in v3:
time: 72.7 us; the launch traced here: 72.5 us
  Pallas kernels  70 us (96%)
  matrix products  2.52 us (3%)
    pallas_call x1, Pallas kernels, on_device(): pl.pallas_call(functools.partial(exchange, shape), out_shape=(jax.ShapeDt...  70 us
    dot_general x1, matrix products, dot(): lax.dot_general(first, second, (dims, ((), ())), precision=precision, pre...  2.52 us

profile of v3, /device:TPU:72, one launch (start us, length us, event | category | flops | bytes accessed | tf_op | source)
XLA Modules:
  0.0 72.5 jit_solution(14017941990256234727)
XLA Ops:
  0.0 0.0 copy-start
  0.0 70.0 %exchange.1 = (bf16[640,128]{1,0:T(8,128)(2,1)}, bf16[128,640]{1,0:T(8,128)(2,1)}) custom-call(f32[640,640]{1,0:T(8,128)} %a_hbm.1), custom_call_target="tpu_custom_call" | custom-call | tf_op jit(solution)/shard_map/exchange/pallas_call | solution.py:412
  70.0 0.0 copy-done
  70.0 2.5 %convolution_subtract_fusion = f32[640,640]{1,0:T(8,128)} fusion(f32[640,640]{1,0:T(8,128)S(1)} %copy-done, bf16[640,128]{1,0:T(8,128)(2,1)} %get-tuple-element.7, bf16[128,640]{1,0:T(8,128)(2,1)} %get-tuple-element.8), kind=kOutput, calls=%fused_computation | convolution fusion | flops 105267200 | bytes 3604480 | tf_op jit(solution)/shard_map/dot_general | solution.py:18
Async XLA Ops:
  0.0 70.0 %copy-start = (f32[640,640]{1,0:T(8,128)S(1)}, f32[640,640]{1,0:T(8,128)}, u32[]{:S(2)}) copy-start(f32[640,640]{1,0:T(8,128)} %a_hbm.1) | copy-start | bytes 4915204

commit v4 on v3

--- a/solution.py
+++ b/solution.py
@@ -24,29 +24,52 @@
     return sorted(range(1, count), key=lambda d: -min(d, count - d))
 
 
+def two_columns(work, i):
+    first = jnp.broadcast_to(work[:, i : i + 1], work.shape)
+    second = jnp.broadcast_to(work[:, i + 1 : i + 2], work.shape)
+    return first, second
+
+
 def eliminate(gram):
     rows = lax.broadcasted_iota(jnp.int32, (PW, PW), 0)
     lanes = lax.broadcasted_iota(jnp.int32, (PW, PW), 1)
+    tall = lax.broadcasted_iota(jnp.int32, (PW, 2 * PW), 0)
     unit = jnp.where(rows == lanes, 1.0, 0.0).astype(F32)
     work = jnp.concatenate([gram, unit], axis=1)
-    for i in range(PW):
-        scale = work[:, i : i + 1] / work[i : i + 1, i : i + 1]
-        work = work - jnp.where(rows[:, :1] > i, scale, 0.0) * work[i : i + 1, :]
+    for i in range(0, PW, 2):
+        first, second = two_columns(work, i)
+        a, b = first[i : i + 1], second[i : i + 1]
+        e, d = first[i + 1 : i + 2], second[i + 1 : i + 2]
+        over_a = 1.0 / a
+        over_q = a / (a * d - b * e)
+        scaled = first * over_a
+        rest = (second - scaled * b) * over_q
+        top, low = work[i : i + 1], work[i + 1 : i + 2]
+        low = low - (e * over_a) * top
+        work = work - jnp.where(tall > i, scaled, 0.0) * top
+        work = work - jnp.where(tall > i + 1, rest, 0.0) * low
     upper, lower = work[:, :PW], work[:, PW:]
     diagonal = jnp.sum(jnp.where(rows == lanes, upper, 0.0), axis=1, keepdims=True)
-    root = jnp.sqrt(diagonal)
-    return jnp.where(lanes >= rows, upper, 0.0) / root, jnp.where(lanes <= rows, lower, 0.0) / root
+    root = 1.0 / jnp.sqrt(diagonal)
+    return jnp.where(lanes >= rows, upper, 0.0) * root, jnp.where(lanes <= rows, lower, 0.0) * root
 
 
 def invert(coupling):
     rows = lax.broadcasted_iota(jnp.int32, (PW, PW), 0)
     lanes = lax.broadcasted_iota(jnp.int32, (PW, PW), 1)
-    tall = lax.broadcasted_iota(jnp.int32, (PW, 1), 0)
+    tall = lax.broadcasted_iota(jnp.int32, (PW, 2 * PW), 0)
     unit = jnp.where(rows == lanes, 1.0, 0.0).astype(F32)
     work = jnp.concatenate([coupling, unit], axis=1)
-    for i in range(PW):
-        pivot = work[i : i + 1, :] / work[i : i + 1, i : i + 1]
-        work = jnp.where(tall == i, pivot, work - work[:, i : i + 1] * pivot)
+    for i in range(0, PW, 2):
+        first, second = two_columns(work, i)
+        a, b = first[i : i + 1], second[i : i + 1]
+        e, d = first[i + 1 : i + 2], second[i + 1 : i + 2]
+        over = 1.0 / (a * d - b * e)
+        top, low = work[i : i + 1], work[i + 1 : i + 2]
+        new_top = (d * over) * top - (b * over) * low
+        new_low = (a * over) * low - (e * over) * top
+        work = work - first * new_top - second * new_low
+        work = jnp.where(tall == i, new_top, jnp.where(tall == i + 1, new_low, work))
     return work[:, PW : 2 * PW]
 
 
@@ -137,6 +160,9 @@
         copy(colp.at[0], lj.at[0], send_c.at[0], recv_b.at[0], partner).start()
         for d in far_first(ny):
             copy(gpart.at[to_y(d)], gs.at[d], send_y.at[1, d], recv_y.at[1, d], at_y(d)).start()
+        for d in far_first(nz):
+            copy(colp.at[1], lj.at[1], send_z.at[2, d], recv_b.at[3], at_z(d)).start()
+        copy(colp.at[1], lj.at[1], send_c.at[2], recv_b.at[3], partner).start()
 
     @pl.when(col == 0)
     def _():
@@ -176,15 +202,18 @@
     def _():
         got(li.at[y], recv_x.at[0, 0])
 
+    def hand_out(which):
+        @pl.when(which)
+        def _():
+            for d in far_first(ny):
+                copy(li.at[y], li.at[y], send_y.at[2, d], recv_y.at[2, d], at_y(d)).start()
+
     @pl.when(col == 0)
     def _():
         for d in far_first(ny):
             copy(rowp.at[0], li.at[0], send_y.at[2, d], recv_y.at[2, d], at_y(d)).start()
 
-    @pl.when(col != 0)
-    def _():
-        for d in far_first(ny):
-            copy(li.at[y], li.at[y], send_y.at[2, d], recv_y.at[2, d], at_y(d)).start()
+    hand_out((col != 0) & (y < ny // 2))
 
     @pl.when((row != 0) & (c == 0))
     def _():
@@ -207,9 +236,6 @@
         for d in far_first(nz):
             copy(g, g, send_z.at[1, d], recv_b.at[1], at_z(d)).start()
         copy(g, g, send_c.at[1], recv_b.at[1], partner).start()
-        for d in far_first(nz):
-            copy(colp.at[1], lj.at[1], send_z.at[2, d], recv_b.at[3], at_z(d)).start()
-        copy(colp.at[1], lj.at[1], send_c.at[2], recv_b.at[3], partner).start()
 
     total = zp[y]
     for d in range(1, ny):
@@ -219,9 +245,18 @@
     for d in range(1, nx):
         copy(zr, zx.at[d], send_x.at[2, d], recv_x.at[2, d], at_x(d)).start()
 
-    for d in range(1, ny):
-        got(li.at[from_y(d)], recv_y.at[2, d])
-    panel = li[...].reshape(2 * PW, size)
+    hand_out(y >= ny // 2)
+
+    def panel_from(upper_half):
+        for d in range(1, ny):
+            there = from_y(d)
+
+            @pl.when((there >= ny // 2) == upper_half)
+            def _():
+                got(li.at[there], recv_y.at[2, d])
+
+    panel_from(False)
+    panel_l = li[: ny // 2].reshape(PW, size)
 
     for d in range(1, nx):
         got(zx.at[d], recv_x.at[2, d])
@@ -230,13 +265,19 @@
     for d in far_first(ny):
         copy(zi.at[y], zi.at[y], send_y.at[5, d], recv_y.at[5, d], at_y(d)).start()
 
-    mine = dot(total, panel.astype(F32), ((1,), (1,)), HIGHEST)
+    mine = dot(total, panel_l.astype(F32), ((1,), (1,)), HIGHEST)
+    mine = jnp.concatenate([mine, mine], axis=1)
     kp[...] = mine
     for d in far_first(nz):
         copy(kp, ks.at[d], send_k.at[d], recv_k.at[d], at_z(d)).start()
 
     @pl.when((row != 0) & (c == 0))
     def _():
+        got(lj.at[1], recv_b.at[3])
+        copy(lj.at[1], lj.at[1], send_c.at[2], recv_b.at[3], partner).start()
+
+    @pl.when((row != 0) & (c == 0))
+    def _():
         got(g, recv_b.at[1])
         copy(g, g, send_c.at[1], recv_b.at[1], partner).start()
 
@@ -245,9 +286,16 @@
         got(g, recv_b.at[1])
 
     whole = g[...].reshape(2 * PW, 2 * PW)
-    gram, cross = whole[:PW, :PW], whole[:PW, PW:]
-    top, top_right = whole[PW:, :PW], whole[PW:, PW:]
-    upper, inverse_t = eliminate(gram)
+    gram, top = whole[:PW, :PW], whole[PW:, :PW]
+    rows = lax.broadcasted_iota(jnp.int32, (PW, PW), 0)
+    lanes = lax.broadcasted_iota(jnp.int32, (PW, PW), 1)
+    on_diagonal = jnp.where(rows == lanes, gram, 0.0)
+    diagonal = jnp.sum(on_diagonal, axis=0, keepdims=True)
+    across = 1.0 / jnp.sqrt(diagonal)
+    down = 1.0 / jnp.sqrt(jnp.sum(on_diagonal, axis=1, keepdims=True))
+    unit_upper, inverse_t = eliminate(gram * down * across)
+    upper = unit_upper * (diagonal * across)
+    inverse_t = inverse_t * across
 
     for d in range(1, ny):
         got(zi.at[from_y(d)], recv_y.at[5, d])
@@ -268,15 +316,6 @@
     kz[...] = mine
     copy(kz, kc, send_c.at[3], recv_c.at[0], partner).start()
 
-    shifted = top + upper
-    coupling = dot(shifted, upper, ((0,), (0,)), HIGHEST)
-    corner = shifted.astype(BF16)
-    change = corner.astype(F32) - top.astype(BF16).astype(F32)
-    side = dot(cross, change, ((1,), (0,)), HIGHEST)
-    side = side + dot(change, cross, ((0,), (1,)), HIGHEST)
-    inner = dot(top_right, change, ((1,), (0,)), HIGHEST)
-    side = side + dot(change, inner, ((0,), (0,)), HIGHEST)
-
     got(kc, recv_c.at[0])
     mine += kc[...]
     kf[...] = mine
@@ -284,47 +323,61 @@
         copy(kf, kk.at[y], send_y.at[6, d], recv_y.at[6, d], at_y(d)).start()
     kk[y] = mine
 
-    @pl.when((row != 0) & (c == 0))
+    shifted = top + upper
+    coupling = dot(shifted * across, unit_upper, ((0,), (0,)), HIGHEST)
+    core = invert(coupling) * down * across
+    corner = shifted.astype(BF16)
+    change = corner.astype(F32) - top.astype(BF16).astype(F32)
+    corner_t = corner.astype(F32).T
+    inner = dot(whole[:, PW:], change, ((1,), (0,)), HIGHEST)
+    side = inner[:PW] + inner[:PW].T + dot(change, inner[PW:], ((0,), (0,)), HIGHEST)
+    mixed = dot(jnp.concatenate([upper, change], axis=0), core, ((1,), (0,)), HIGHEST)
+
+    panel_from(True)
+    panel_t = li[ny // 2 :].reshape(PW, size)
+
+    @pl.when(c == 1)
     def _():
         got(lj.at[1], recv_b.at[3])
-        copy(lj.at[1], lj.at[1], send_c.at[2], recv_b.at[3], partner).start()
-
-    @pl.when(c == 1)
-    def _():
-        got(lj.at[1], recv_b.at[3])
-
-    core = invert(coupling)
-    corner_t = corner.astype(F32).T
-    basis_i = basis_of(panel[:PW], corner_t, row == 0).astype(F32).T
+
+    basis_i = basis_of(panel_l, corner_t, row == 0)
     basis_j = basis_of(lj[0], corner_t, col == 0)
+    left_out[:, :PW] = basis_i.T
     right_out[PW:, :] = basis_j
-    shift = dot(change, core, ((1,), (0,)), HIGHEST)
-    first_i = dot(core, images, ((0,), (0,)), HIGHEST)
-    first_i = first_i + dot(shift, panel[PW:].astype(F32), ((0,), (0,)), HIGHEST)
-    first_i = first_i.T
-    shift_j = dot(shift, lj[1].astype(F32), ((0,), (0,)), HIGHEST)
-    scaled = dot(upper, core, ((1,), (0,)), HIGHEST)
+    high = images.astype(BF16)
+    low = (images - high.astype(F32)).astype(BF16)
+    stack_i = jnp.concatenate([high, low, panel_t, basis_i], axis=0)
+    stack_tb = jnp.concatenate([lj[1], basis_j], axis=0)
+
+    @pl.when((row != col) & (c == col % 2))
+    def _():
+        got(zj, recv_b.at[4])
+        copy(zj, zj, send_d.at[0], recv_b.at[4], partner).start()
 
     for d in range(1, ny):
         got(kk.at[from_y(d)], recv_y.at[6, d])
     projection = kk[...].reshape(PW, 2 * PW)[:, :PW] + side
     middle = dot(core, projection, ((0,), (0,)), HIGHEST)
-    middle = 0.5 * dot(middle, core, ((1,), (0,)), HIGHEST)
-    update_i = first_i - dot(basis_i, middle, ((1,), (0,)), HIGHEST)
-    left_out[...] = jnp.concatenate([basis_i, update_i], axis=1).astype(BF16)
-    shift_j = shift_j - dot(middle, basis_j.astype(F32), ((0,), (0,)), HIGHEST)
-
-    @pl.when((row != col) & (c == col % 2))
+    middle = -0.5 * dot(middle, core, ((1,), (0,)), HIGHEST)
+
+    def weigh(weights, stack):
+        tall = weights.T
+        first = tall.astype(BF16)
+        rest = tall - first.astype(F32)
+        second = rest.astype(BF16)
+        third = (rest - second.astype(F32)).astype(BF16)
+        parts = dot(jnp.concatenate([first, second, third], axis=0), stack, ((1,), (0,)))
+        return (parts[:PW] + (parts[PW : 2 * PW] + parts[2 * PW :])).astype(BF16)
+
+    weights_i = jnp.concatenate([core, core, mixed[PW:], middle], axis=0)
+    left_out[:, PW:] = weigh(weights_i, stack_i).T
+
+    @pl.when(c != col % 2)
     def _():
         got(zj, recv_b.at[4])
-        copy(zj, zj, send_d.at[0], recv_b.at[4], partner).start()
-
-    @pl.when(c != col % 2)
-    def _():
-        got(zj, recv_b.at[4])
-
-    first_j = dot(scaled, zj[...].astype(F32), ((0,), (0,)), HIGHEST)
-    right_out[:PW, :] = (first_j + shift_j).astype(BF16)
+
+    weights_j = jnp.concatenate([mixed, middle], axis=0)
+    right_out[:PW, :] = weigh(weights_j, jnp.concatenate([zj[...], stack_tb], axis=0))
 
     for d in range(1, ny):
         sent(li.at[0], send_y.at[2, d])
@@ -373,6 +426,10 @@
     def _():
         for d in range(1, nz):
             sent(zh, send_d.at[d])
+
+
+def subtract(a_ref, left_ref, right_ref, out_ref):
+    out_ref[...] = a_ref[...] - dot(left_ref[...], right_ref[...], ((1,), (0,)))
 
 
 def on_device(shape, matrix):
@@ -412,8 +469,8 @@
     left, right = pl.pallas_call(
         functools.partial(exchange, shape),
         out_shape=(
-            jax.ShapeDtypeStruct((size, 2 * PW), BF16),
-            jax.ShapeDtypeStruct((2 * PW, size), BF16),
+            pltpu.VMEM((size, 2 * PW), BF16),
+            pltpu.VMEM((2 * PW, size), BF16),
         ),
         in_specs=[pl.BlockSpec(memory_space=pl.ANY)],
         out_specs=(vmem, vmem),

time: 72.7 us -> 64.4 us (0.89)
  the two profiles are of different devices: /device:TPU:72 before, /device:TPU:70 now
where the time goes in v4:
time: 64.4 us; the launch traced here: 64.2 us
  Pallas kernels  62.7 us (97%)
  matrix products  1.52 us (2%)
    pallas_call x1, Pallas kernels, on_device(): pl.pallas_call(functools.partial(exchange, shape), out_shape=(pltpu.VMEM(...  62.7 us
    dot_general x1, matrix products, dot(): lax.dot_general(first, second, (dims, ((), ())), precision=precision, pre...  1.52 us

profile of v4, /device:TPU:70, one launch (start us, length us, event | category | flops | bytes accessed | tf_op | source)
XLA Modules:
  0.0 64.2 jit_solution(8359440304567820622)
XLA Ops:
  0.0 0.0 copy-start
  0.0 62.7 %exchange.1 = (bf16[640,128]{1,0:T(8,128)(2,1)S(1)}, bf16[128,640]{1,0:T(8,128)(2,1)S(1)}) custom-call(f32[640,640]{1,0:T(8,128)} %a_hbm.1), custom_call_target="tpu_custom_call" | custom-call | tf_op jit(solution)/shard_map/exchange/pallas_call | solution.py:469
  62.7 0.0 copy-done
  62.7 1.5 %convolution_subtract_fusion = f32[640,640]{1,0:T(8,128)} fusion(f32[640,640]{1,0:T(8,128)S(1)} %copy-done, bf16[640,128]{1,0:T(8,128)(2,1)S(1)} %get-tuple-element.7, bf16[128,640]{1,0:T(8,128)(2,1)S(1)} %get-tuple-element.8), kind=kOutput, calls=%fused_computation | convolution fusion | flops 105267200 | bytes 3604480 | tf_op jit(solution)/shard_map/dot_general | solution.py:18
Async XLA Ops:
  0.0 62.7 %copy-start = (f32[640,640]{1,0:T(8,128)S(1)}, f32[640,640]{1,0:T(8,128)}, u32[]{:S(2)}) copy-start(f32[640,640]{1,0:T(8,128)} %a_hbm.1) | copy-start | bytes 4915204

commit v5 on v4

--- a/solution.py
+++ b/solution.py
@@ -82,7 +82,7 @@
 
 def exchange(shape, a_hbm, left_out, right_out,
              a, rowp, colp, gpart,
-             li, lj, zp, zs, zr, zx, zi, zh, zj, gs, gr, gx, g, kp, ks, kz, kc, kf, kk,
+             li, lj, zp, zs, zr, zx, zi, zh, zj, gs, gr, gx, g, kp, ks, kf, kk,
              a_sem, send_z, send_d, send_y, recv_y, send_x, recv_x, send_k, recv_k,
              recv_b, send_c, recv_c):
     nz, nx, ny = shape
@@ -98,6 +98,9 @@
     def at_y(d):
         return (row, x * ny + lax.rem(y + d, ny))
 
+    def across_y(d):
+        return (z * 2 + 1 - c, x * ny + lax.rem(y + d, ny))
+
     def at_x(d):
         return (row, lax.rem(x + d, nx) * ny + y)
 
@@ -124,6 +127,7 @@
     barrier = pltpu.get_barrier_semaphore()
     peers = [at_z(d) for d in range(1, nz)] + [at_y(d) for d in range(1, ny)]
     peers += [at_x(d) for d in range(1, nx)] + [partner]
+    peers += [across_y(d) for d in range(1, ny)]
     for peer in peers:
         pl.semaphore_signal(barrier, inc=1, device_id=peer, device_id_type=MESH)
     fetch.wait()
@@ -262,8 +266,18 @@
         got(zx.at[d], recv_x.at[2, d])
         total += zx[d]
     zi[y] = total
+    gap = lax.rem(row % ny + ny - y, ny)
+    beside = (x == row // ny) & (gap != 0)
+
+    @pl.when(beside)
+    def _():
+        copy(zi.at[y], zi.at[y], send_y.at[5, gap], recv_y.at[5, gap], (row, row)).start()
+
     for d in far_first(ny):
-        copy(zi.at[y], zi.at[y], send_y.at[5, d], recv_y.at[5, d], at_y(d)).start()
+
+        @pl.when(jnp.logical_not(beside & (gap == d)))
+        def _():
+            copy(zi.at[y], zi.at[y], send_y.at[5, d], recv_y.at[5, d], at_y(d)).start()
 
     mine = dot(total, panel_l.astype(F32), ((1,), (1,)), HIGHEST)
     mine = jnp.concatenate([mine, mine], axis=1)
@@ -313,15 +327,12 @@
     for d in range(1, nz):
         got(ks.at[d], recv_k.at[d])
         mine += ks[d]
-    kz[...] = mine
-    copy(kz, kc, send_c.at[3], recv_c.at[0], partner).start()
-
-    got(kc, recv_c.at[0])
-    mine += kc[...]
     kf[...] = mine
     for d in far_first(ny):
-        copy(kf, kk.at[y], send_y.at[6, d], recv_y.at[6, d], at_y(d)).start()
-    kk[y] = mine
+        copy(kf, kk.at[c, y], send_y.at[6, d], recv_y.at[6, d], at_y(d)).start()
+        copy(kf, kk.at[c, y], send_y.at[7, d], recv_y.at[7, d], across_y(d)).start()
+    copy(kf, kk.at[c, y], send_c.at[3], recv_c.at[0], partner).start()
+    kk[c, y] = mine
 
     shifted = top + upper
     coupling = dot(shifted * across, unit_upper, ((0,), (0,)), HIGHEST)
@@ -346,20 +357,6 @@
     right_out[PW:, :] = basis_j
     high = images.astype(BF16)
     low = (images - high.astype(F32)).astype(BF16)
-    stack_i = jnp.concatenate([high, low, panel_t, basis_i], axis=0)
-    stack_tb = jnp.concatenate([lj[1], basis_j], axis=0)
-
-    @pl.when((row != col) & (c == col % 2))
-    def _():
-        got(zj, recv_b.at[4])
-        copy(zj, zj, send_d.at[0], recv_b.at[4], partner).start()
-
-    for d in range(1, ny):
-        got(kk.at[from_y(d)], recv_y.at[6, d])
-    projection = kk[...].reshape(PW, 2 * PW)[:, :PW] + side
-    middle = dot(core, projection, ((0,), (0,)), HIGHEST)
-    middle = -0.5 * dot(middle, core, ((1,), (0,)), HIGHEST)
-
     def weigh(weights, stack):
         tall = weights.T
         first = tall.astype(BF16)
@@ -367,23 +364,42 @@
         second = rest.astype(BF16)
         third = (rest - second.astype(F32)).astype(BF16)
         parts = dot(jnp.concatenate([first, second, third], axis=0), stack, ((1,), (0,)))
-        return (parts[:PW] + (parts[PW : 2 * PW] + parts[2 * PW :])).astype(BF16)
-
-    weights_i = jnp.concatenate([core, core, mixed[PW:], middle], axis=0)
-    left_out[:, PW:] = weigh(weights_i, stack_i).T
+        return parts[:PW] + (parts[PW : 2 * PW] + parts[2 * PW :])
+
+    fixed_i = weigh(
+        jnp.concatenate([core, core, mixed[PW:]], axis=0),
+        jnp.concatenate([high, low, panel_t], axis=0),
+    )
+    fixed_j = weigh(mixed[PW:], lj[1])
+
+    @pl.when((row != col) & (c == col % 2))
+    def _():
+        got(zj, recv_b.at[4])
+        copy(zj, zj, send_d.at[0], recv_b.at[4], partner).start()
+
+    for d in range(1, ny):
+        got(kk.at[c, from_y(d)], recv_y.at[6, d])
+        got(kk.at[1 - c, from_y(d)], recv_y.at[7, d])
+    got(kk.at[1 - c, y], recv_c.at[0])
+    projection = (kk[0] + kk[1]).reshape(PW, 2 * PW)[:, :PW] + side
+    middle = dot(core, projection, ((0,), (0,)), HIGHEST)
+    middle = -0.5 * dot(middle, core, ((1,), (0,)), HIGHEST)
+
+    left_out[:, PW:] = (fixed_i + weigh(middle, basis_i)).astype(BF16).T
+    fixed_j = fixed_j + weigh(middle, basis_j)
 
     @pl.when(c != col % 2)
     def _():
         got(zj, recv_b.at[4])
 
-    weights_j = jnp.concatenate([mixed, middle], axis=0)
-    right_out[:PW, :] = weigh(weights_j, jnp.concatenate([zj[...], stack_tb], axis=0))
+    right_out[:PW, :] = (fixed_j + weigh(mixed[:PW], zj[...])).astype(BF16)
 
     for d in range(1, ny):
         sent(li.at[0], send_y.at[2, d])
         sent(zr, send_y.at[3, d])
         sent(zr, send_y.at[5, d])
         sent(kp, send_y.at[6, d])
+        sent(kp, send_y.at[7, d])
     for d in range(1, nx):
         sent(zr, send_x.at[2, d])
     for d in range(1, nz):
@@ -458,10 +474,8 @@
         pltpu.VMEM((low, 2 * PW), F32),
         pltpu.VMEM((nz, low, 2 * PW), F32),
         pltpu.VMEM((low, 2 * PW), F32),
-        pltpu.VMEM((low, 2 * PW), F32),
-        pltpu.VMEM((low, 2 * PW), F32),
-        pltpu.VMEM((ny, low, 2 * PW), F32),
-        dma((1,)), dma((3, nz)), dma((nz,)), dma((7, ny)), dma((7, ny)),
+        pltpu.VMEM((2, ny, low, 2 * PW), F32),
+        dma((1,)), dma((3, nz)), dma((nz,)), dma((8, ny)), dma((8, ny)),
         dma((3, nx)), dma((3, nx)), dma((nz,)), dma((nz,)),
         dma((5,)), dma((4,)), dma((1,)),
     ]

time: 64.4 us -> 63.1 us (0.980)
  Pallas kernels: 62.7 us -> 61.4 us
    pallas_call x1, Pallas kernels: 62.7 us -> 61.4 us  [on_device(): pl.pallas_call(functools.partial(exchange, shape), out_shape=(pltpu.VMEM(...]
where the time goes in v5:
time: 63.1 us; the launch traced here: 62.9 us
  Pallas kernels  61.4 us (97%)
  matrix products  1.52 us (2%)
    pallas_call x1, Pallas kernels, on_device(): pl.pallas_call(functools.partial(exchange, shape), out_shape=(pltpu.VMEM(...  61.4 us
    dot_general x1, matrix products, dot(): lax.dot_general(first, second, (dims, ((), ())), precision=precision, pre...  1.52 us

profile of v5, /device:TPU:70, one launch (start us, length us, event | category | flops | bytes accessed | tf_op | source)
XLA Modules:
  0.0 62.9 jit_solution(223366008202462436)
XLA Ops:
  0.0 0.0 copy-start
  0.0 61.4 %exchange.1 = (bf16[640,128]{1,0:T(8,128)(2,1)S(1)}, bf16[128,640]{1,0:T(8,128)(2,1)S(1)}) custom-call(f32[640,640]{1,0:T(8,128)} %a_hbm.1), custom_call_target="tpu_custom_call" | custom-call | tf_op jit(solution)/shard_map/exchange/pallas_call | solution.py:483
  61.4 0.0 copy-done
  61.4 1.5 %convolution_subtract_fusion = f32[640,640]{1,0:T(8,128)} fusion(f32[640,640]{1,0:T(8,128)S(1)} %copy-done, bf16[640,128]{1,0:T(8,128)(2,1)S(1)} %get-tuple-element.7, bf16[128,640]{1,0:T(8,128)(2,1)S(1)} %get-tuple-element.8), kind=kOutput, calls=%fused_computation | convolution fusion | flops 105267200 | bytes 3604480 | tf_op jit(solution)/shard_map/dot_general | solution.py:18
Async XLA Ops:
  0.0 61.4 %copy-start = (f32[640,640]{1,0:T(8,128)S(1)}, f32[640,640]{1,0:T(8,128)}, u32[]{:S(2)}) copy-start(f32[640,640]{1,0:T(8,128)} %a_hbm.1) | copy-start | bytes 4915204

commit v6 on v5

--- a/solution.py
+++ b/solution.py
@@ -22,6 +22,13 @@
 
 def far_first(count):
     return sorted(range(1, count), key=lambda d: -min(d, count - d))
+
+
+def in_parts(value):
+    first = value.astype(BF16).astype(F32)
+    rest = value - first
+    second = rest.astype(BF16).astype(F32)
+    return jnp.concatenate([first, second, rest - second], axis=0).astype(BF16)
 
 
 def two_columns(work, i):
@@ -81,7 +88,7 @@
 
 
 def exchange(shape, a_hbm, left_out, right_out,
-             a, rowp, colp, gpart,
+             a, a_half, rowp, colp, gpart,
              li, lj, zp, zs, zr, zx, zi, zh, zj, gs, gr, gx, g, kp, ks, kf, kk,
              a_sem, send_z, send_d, send_y, recv_y, send_x, recv_x, send_k, recv_k,
              recv_b, send_c, recv_c):
@@ -131,6 +138,7 @@
     for peer in peers:
         pl.semaphore_signal(barrier, inc=1, device_id=peer, device_id_type=MESH)
     fetch.wait()
+    a_half[...] = a[...].astype(BF16)
 
     bands = lax.broadcasted_iota(jnp.int32, (2 * PW, size), 0)
     places = lax.broadcasted_iota(jnp.int32, (2 * PW, size), 1)
@@ -228,7 +236,7 @@
     def _():
         got(lj.at[0], recv_b.at[0])
 
-    part = dot(lj[0], a[...].astype(BF16), ((1,), (1,)))
+    part = dot(lj[0], a_half[...], ((1,), (1,)))
     zp[...] = part.reshape(zp.shape)
     for d in far_first(ny):
         copy(zp.at[to_y(d)], zs.at[d], send_y.at[3, d], recv_y.at[3, d], at_y(d)).start()
@@ -279,8 +287,10 @@
         def _():
             copy(zi.at[y], zi.at[y], send_y.at[5, d], recv_y.at[5, d], at_y(d)).start()
 
-    mine = dot(total, panel_l.astype(F32), ((1,), (1,)), HIGHEST)
-    mine = jnp.concatenate([mine, mine], axis=1)
+    mine = dot(in_parts(total), panel_l, ((1,), (1,)))
+    low = total.shape[0]
+    mine = mine[:low] + (mine[low : 2 * low] + mine[2 * low :])
+    mine = jnp.concatenate([mine[: low // 2], mine[low // 2 :]], axis=1)
     kp[...] = mine
     for d in far_first(nz):
         copy(kp, ks.at[d], send_k.at[d], recv_k.at[d], at_z(d)).start()
@@ -356,19 +366,14 @@
     left_out[:, :PW] = basis_i.T
     right_out[PW:, :] = basis_j
     high = images.astype(BF16)
-    low = (images - high.astype(F32)).astype(BF16)
+    below = (images - high.astype(F32)).astype(BF16)
     def weigh(weights, stack):
-        tall = weights.T
-        first = tall.astype(BF16)
-        rest = tall - first.astype(F32)
-        second = rest.astype(BF16)
-        third = (rest - second.astype(F32)).astype(BF16)
-        parts = dot(jnp.concatenate([first, second, third], axis=0), stack, ((1,), (0,)))
+        parts = dot(in_parts(weights.T), stack, ((1,), (0,)))
         return parts[:PW] + (parts[PW : 2 * PW] + parts[2 * PW :])
 
     fixed_i = weigh(
         jnp.concatenate([core, core, mixed[PW:]], axis=0),
-        jnp.concatenate([high, low, panel_t], axis=0),
+        jnp.concatenate([high, below, panel_t], axis=0),
     )
     fixed_j = weigh(mixed[PW:], lj[1])
 
@@ -381,7 +386,9 @@
         got(kk.at[c, from_y(d)], recv_y.at[6, d])
         got(kk.at[1 - c, from_y(d)], recv_y.at[7, d])
     got(kk.at[1 - c, y], recv_c.at[0])
-    projection = (kk[0] + kk[1]).reshape(PW, 2 * PW)[:, :PW] + side
+    halves = kk[0] + kk[1]
+    halves = jnp.concatenate([halves[:, :, :PW], halves[:, :, PW:]], axis=1)
+    projection = halves.reshape(PW, PW) + side
     middle = dot(core, projection, ((0,), (0,)), HIGHEST)
     middle = -0.5 * dot(middle, core, ((1,), (0,)), HIGHEST)
 
@@ -455,6 +462,7 @@
     dma = pltpu.SemaphoreType.DMA
     scratch = [
         pltpu.VMEM((size, size), F32),
+        pltpu.VMEM((size, size), BF16),
         pltpu.VMEM((ny, tall, size), BF16),
         pltpu.VMEM((2, PW, size), BF16),
         pltpu.VMEM((ny, tall, 2 * PW), F32),
@@ -471,10 +479,10 @@
         pltpu.VMEM((tall, 2 * PW), F32),
         pltpu.VMEM((nx, tall, 2 * PW), F32),
         pltpu.VMEM((ny, tall, 2 * PW), F32),
-        pltpu.VMEM((low, 2 * PW), F32),
-        pltpu.VMEM((nz, low, 2 * PW), F32),
-        pltpu.VMEM((low, 2 * PW), F32),
-        pltpu.VMEM((2, ny, low, 2 * PW), F32),
+        pltpu.VMEM((low // 2, 2 * PW), F32),
+        pltpu.VMEM((nz, low // 2, 2 * PW), F32),
+        pltpu.VMEM((low // 2, 2 * PW), F32),
+        pltpu.VMEM((2, ny, low // 2, 2 * PW), F32),
         dma((1,)), dma((3, nz)), dma((nz,)), dma((8, ny)), dma((8, ny)),
         dma((3, nx)), dma((3, nx)), dma((nz,)), dma((nz,)),
         dma((5,)), dma((4,)), dma((1,)),

time: 63.1 us -> 62.6 us (level)
  the two profiles are of different devices: /device:TPU:70 before, /device:TPU:1 now
where the time goes in v6:
time: 62.6 us; the launch traced here: 62.4 us
  Pallas kernels  60.9 us (97%)
  matrix products  1.52 us (2%)
    pallas_call x1, Pallas kernels, on_device(): pl.pallas_call(functools.partial(exchange, shape), out_shape=(pltpu.VMEM(...  60.9 us
    dot_general x1, matrix products, dot(): lax.dot_general(first, second, (dims, ((), ())), precision=precision, pre...  1.52 us

profile of v6, /device:TPU:1, one launch (start us, length us, event | category | flops | bytes accessed | tf_op | source)
XLA Modules:
  0.0 62.4 jit_solution(10885801868946242736)
XLA Ops:
  0.0 0.0 copy-start
  0.0 60.9 %exchange.1 = (bf16[640,128]{1,0:T(8,128)(2,1)S(1)}, bf16[128,640]{1,0:T(8,128)(2,1)S(1)}) custom-call(f32[640,640]{1,0:T(8,128)} %a_hbm.1), custom_call_target="tpu_custom_call" | custom-call | tf_op jit(solution)/shard_map/exchange/pallas_call | solution.py:491
  60.9 0.0 copy-done
  60.9 1.5 %convolution_subtract_fusion = f32[640,640]{1,0:T(8,128)} fusion(f32[640,640]{1,0:T(8,128)S(1)} %copy-done, bf16[640,128]{1,0:T(8,128)(2,1)S(1)} %get-tuple-element.7, bf16[128,640]{1,0:T(8,128)(2,1)S(1)} %get-tuple-element.8), kind=kOutput, calls=%fused_computation | convolution fusion | flops 105267200 | bytes 3604480 | tf_op jit(solution)/shard_map/dot_general | solution.py:18
Async XLA Ops:
  0.0 60.9 %copy-start = (f32[640,640]{1,0:T(8,128)S(1)}, f32[640,640]{1,0:T(8,128)}, u32[]{:S(2)}) copy-start(f32[640,640]{1,0:T(8,128)} %a_hbm.1) | copy-start | bytes 4915204
